TPU v7x, 128 devices: a whole 4x4x4 slice. The times are simulated.
128 devices in a mesh: dev: 128 (over z, x, y, core).
Axes of the slice: x: 4, y: 4, z: 4, core: 2. Of those that a mesh axis runs over, the one named last changes fastest.
Arguments:
- cotangent: bfloat16 [32768, 2048], P('dev'), may hold values from -6 to 6
- hot_table: bfloat16 [2048, 128], replicated, may hold values from -6 to 6
- cold_table: float32 [262144, 128], P('dev'), may hold values from -6 to 6
- cold_m: float32 [262144, 128], P('dev'), may hold values from -0.75 to 0.75
- cold_v: float32 [262144, 128], P('dev'), may hold values from 0.0001 to 0.01
- cross_down: bfloat16 [2048, 512], replicated, may hold values from -0.125 to 0.125
- cross_up: bfloat16 [512, 2048], replicated, may hold values from -0.25 to 0.25
- cross_bias: float32 [2048], replicated, may hold values from -6 to 6
- dense_master: float32 [2048, 1024], P('dev'), may hold values from -0.4375 to 0.4375
- dense_m: float32 [2048, 1024], P('dev'), may hold values from -6 to 6
- dense_v: float32 [2048, 1024], P('dev'), may hold values from 1 to 30
- hot_ids: int32 [32768, 16], P('dev'), may hold values from 0 to 2047
- lookup_slot: int32 [32768, 16], P('dev'), may hold values from -1 to 3071, as said below
- fetch_rows: int32 [128, 128, 24], P('dev'), may hold values from 0 to 2047, as said below
Outputs:
- hot_grad: float32 [2048, 128], replicated
- bias_grad: float32 [2048], replicated
- cold_new: float32 [262144, 128], P('dev')
- cold_m_new: float32 [262144, 128], P('dev')
- cold_v_new: float32 [262144, 128], P('dev')
- master_new: float32 [2048, 1024], P('dev')
- dense_m_new: float32 [2048, 1024], P('dev')
- dense_v_new: float32 [2048, 1024], P('dev')
- new_weights: bfloat16 [2048, 1024], replicated
Inputs may be any that keep to these rules, and one draw needn't show every extreme that they name: `lookup_slot`: -1 marks a hot lookup; any other value o * 24 + s reads slot s of the list that the lookup's device sends to owner o. For each device and owner the slots read are 0 to c - 1 for some c of at most 24, each read by exactly one lookup of that device; every device reads 24 slots from some owner, and some owner is read 24 slots by every device. `fetch_rows`: slots that no lookup reads still name rows.
All inputs are finite; a program needn't handle non-finite values.
Results may differ from a plain program's by a relative error of at most 0.0055.
Values may be sent and summed in bfloat16 or wider, within the bound.
A program may use at most 128 MiB of HBM per device.

v0:
```python
import jax
import jax.numpy as jnp
from jax import lax
from jax.sharding import PartitionSpec as P

first_decay = 0.9
second_decay = 0.999
adam_epsilon = 1e-08
learn_rate = 0.01
first_fix = 1.0 - (0.9**10) ** 10
second_fix = 1.0 - (0.999**10) ** 10


def adam_update(params, moment_one, moment_two, gradient):
    moment_one = first_decay * moment_one + (1.0 - first_decay) * gradient
    moment_two = second_decay * moment_two + (1.0 - second_decay) * gradient * gradient
    params = params - learn_rate * (moment_one / first_fix) / (
        jnp.sqrt(moment_two / second_fix) + adam_epsilon
    )
    return (params, moment_one, moment_two)


def body(
    cotangent,
    hot_table,
    cold_table,
    cold_m,
    cold_v,
    cross_down,
    cross_up,
    cross_bias,
    dense_master,
    dense_m,
    dense_v,
    hot_ids,
    lookup_slot,
    fetch_rows,
):
    devices = lax.axis_size("dev")
    sample_count, fields = hot_ids.shape
    slab_rows, emb_width = cold_table.shape
    hot_rows = hot_table.shape[0]
    capacity = fetch_rows.shape[2]
    cross_width = cross_down.shape[0]
    shard_rows = dense_master.shape[0]
    scale_mean = 1.0 / devices
    requests = lax.all_to_all(fetch_rows, "dev", split_axis=1, concat_axis=0, tiled=True)
    request_flat = requests.reshape(devices * capacity)
    picked = jnp.take(cold_table, request_flat, axis=0).astype(jnp.bfloat16)
    fetched = lax.all_to_all(
        picked.reshape(devices, capacity, emb_width), "dev", split_axis=0, concat_axis=0, tiled=True
    )
    fetched_flat = fetched.reshape(devices * capacity, emb_width)
    is_hot = lookup_slot < 0
    cold_pos = jnp.maximum(lookup_slot, 0)
    chosen = jnp.where(
        is_hot[..., None],
        jnp.take(hot_table, hot_ids, axis=0),
        jnp.take(fetched_flat, cold_pos, axis=0),
    )
    inputs = chosen.reshape(sample_count, cross_width)
    latent = jnp.dot(inputs, cross_down, preferred_element_type=jnp.float32).astype(jnp.bfloat16)
    mixing = jnp.dot(latent, cross_up, preferred_element_type=jnp.float32) + cross_bias
    grad_f32 = cotangent.astype(jnp.float32)
    grad_mix = (grad_f32 * inputs.astype(jnp.float32)).astype(jnp.bfloat16)
    grad_latent = lax.dot_general(
        grad_mix, cross_up, (((1,), (1,)), ((), ())), preferred_element_type=jnp.float32
    ).astype(jnp.bfloat16)
    back_part = lax.dot_general(
        grad_latent, cross_down, (((1,), (1,)), ((), ())), preferred_element_type=jnp.float32
    )
    grad_input = grad_f32 * (mixing + 1.0) + back_part
    per_lookup = grad_input.reshape(sample_count * fields, emb_width)
    cold_target = jnp.where(is_hot, devices * capacity, lookup_slot).reshape(-1)
    cold_part = (
        jnp.zeros((devices * capacity, emb_width), jnp.float32)
        .at[cold_target]
        .add(per_lookup, mode="drop")
    )
    returned = lax.all_to_all(
        cold_part.reshape(devices, capacity, emb_width).astype(jnp.bfloat16),
        "dev",
        split_axis=0,
        concat_axis=0,
        tiled=True,
    ).astype(jnp.float32)
    cold_sum = (
        jnp.zeros((slab_rows, emb_width), jnp.float32)
        .at[request_flat]
        .add(returned.reshape(devices * capacity, emb_width))
    )
    cold_new, cold_m_new, cold_v_new = adam_update(
        cold_table, cold_m, cold_v, cold_sum * scale_mean
    )
    hot_target = jnp.where(is_hot, hot_ids, hot_rows).reshape(-1)
    hot_part = (
        jnp.zeros((hot_rows, emb_width), jnp.float32).at[hot_target].add(per_lookup, mode="drop")
    )
    bias_part = jnp.sum(grad_mix.astype(jnp.float32), axis=0)
    down_part = lax.dot_general(
        inputs, grad_latent, (((0,), (0,)), ((), ())), preferred_element_type=jnp.float32
    )
    up_part = lax.dot_general(
        grad_mix, latent, (((0,), (0,)), ((), ())), preferred_element_type=jnp.float32
    )
    dense_total, hot_sum, bias_sum = lax.psum(
        (jnp.concatenate([down_part, up_part], axis=1), hot_part, bias_part), "dev"
    )
    dense_own = lax.dynamic_slice_in_dim(
        dense_total, lax.axis_index("dev") * shard_rows, shard_rows, 0
    )
    master_new, dense_m_new, dense_v_new = adam_update(
        dense_master, dense_m, dense_v, dense_own * scale_mean
    )
    new_weights = lax.all_gather(master_new.astype(jnp.bfloat16), "dev", axis=0, tiled=True)
    return (
        hot_sum * scale_mean,
        bias_sum * scale_mean,
        cold_new,
        cold_m_new,
        cold_v_new,
        master_new,
        dense_m_new,
        dense_v_new,
        new_weights,
    )


def solution(mesh):
    return jax.shard_map(
        body,
        mesh=mesh,
        in_specs=(
            P("dev", None),
            P(),
            P("dev", None),
            P("dev", None),
            P("dev", None),
            P(),
            P(),
            P(),
            P("dev", None),
            P("dev", None),
            P("dev", None),
            P("dev", None),
            P("dev", None),
            P("dev", None, None),
        ),
        out_specs=(
            P(),
            P(),
            P("dev", None),
            P("dev", None),
            P("dev", None),
            P("dev", None),
            P("dev", None),
            P("dev", None),
            P(),
        ),
        check_vma=False,
    )
```

profile of v0, /device:TPU:1, one launch (start us, length us, event | category | flops | bytes accessed | tf_op | source)
XLA Modules:
  0.0 444.6 jit_solution(1659322300274573005)
XLA Ops:
  7.2 0.0 copy-start
  7.2 1.6 copy.76
  8.8 11.5 %all-to-all-start = ((s32[1,128,24]{2,0,1:T(1,128)}), s32[1,128,24]{2,0,1:T(1,128)S(1)}, u32[]{:S(2)}, u32[]{:S(2)}) async-start(s32[1,128,24]{2,0,1:T(1,128)} %copy.76), calls=%async_computation | async-start | bytes 131072 | tf_op jit(solution)/shard_map/all_to_all | solution.py:47
  20.3 0.7 compare_and_fusion.1
  21.0 0.7 broadcast_select_fusion
  21.7 0.7 compare_select_fusion.4
  22.5 0.1 copy.74
  22.6 0.1 reshape.179
  22.7 0.1 copy.77
  22.8 0.1 reshape.195
  22.9 0.7 broadcast_compare_fusion
  23.6 0.1 copy.72
  23.8 0.1 copy.75
  23.9 0.1 copy.73
  24.0 0.1 copy.71
  24.1 0.1 reshape.167
  24.2 15.0 %gather_fusion = bf16[4096,128]{1,0:T(8,128)(2,1)} fusion(bf16[2048,128]{1,0:T(8,128)(2,1)S(1)} %copy-done.1, s32[4096]{0:T(1024)S(1)} %broadcast_clamp_fusion.1), kind=kCustom, calls=%fused_computation | custom fusion | bytes 2113536 | tf_op jit(solution)/shard_map/jit(_take)/gather | solution.py:58
  39.3 0.0 all-to-all-done
  39.3 0.5 broadcast.134
  39.8 0.8 reduce.3
  40.6 0.1 reshape.169
  40.8 9.5 %gather_fusion.1 = bf16[3072,128]{1,0:T(8,128)(2,1)S(1)} fusion(f32[2048,128]{1,0:T(8,128)} %param.16, s32[3072]{0:T(1024)S(1)} %broadcast_clamp_fusion.2), kind=kCustom, calls=%fused_computation.1 | custom fusion | bytes 1585152 | tf_op jit(solution)/shard_map/jit(_take)/gather | solution.py:49
  50.3 1.3 select_convert_fusion
  51.7 9.8 %all-to-all-start.1 = ((bf16[128,24,128]{2,1,0:T(8,128)(2,1)}), bf16[128,24,128]{2,1,0:T(8,128)(2,1)S(1)}, u32[]{:S(2)}, u32[]{:S(2)}) async-start(bf16[128,24,128]{2,1,0:T(8,128)(2,1)} %select_convert_fusion), calls=%async_computation.1 | async-start | bytes 1572864 | tf_op jit(solution)/shard_map/all_to_all | solution.py:50
  61.4 0.0 all-reduce.3.cloned.1.call-start
  61.5 16.1 %all-to-all-done.1 = bf16[128,24,128]{2,1,0:T(8,128)(2,1)S(1)} async-done(((bf16[128,24,128]{2,1,0:T(8,128)(2,1)}), bf16[128,24,128]{2,1,0:T(8,128)(2,1)S(1)}, u32[]{:S(2)}, u32[]{:S(2)}) %all-to-all-start.1) | async-done | bytes 786464 | tf_op jit(solution)/shard_map/all_to_all | solution.py:50
  77.6 15.0 %gather_fusion.2 = bf16[4096,128]{1,0:T(8,128)(2,1)} fusion(bf16[3072,128]{1,0:T(8,128)(2,1)S(1)} %bitcast.31, s32[4096]{0:T(1024)S(1)} %broadcast_clamp_fusion), kind=kCustom, calls=%fused_computation.2 | custom fusion | bytes 2113536 | tf_op jit(solution)/shard_map/jit(_take)/gather | solution.py:59
  92.7 5.5 %select_select_fusion = bf16[256,16,128]{2,1,0:T(8,128)(2,1)S(1)} fusion(bf16[256,16,128]{2,1,0:T(8,128)(2,1)} %bitcast.38, bf16[256,16,128]{2,1,0:T(8,128)(2,1)} %bitcast.37, pred[256,16]{1,0:T(8,128)(4,1)S(1)} %copy.75, pred[256,16]{1,0:T(8,128)(4,1)S(1)} %copy.73, pred[256,16]{1,0:T(8,128)(4,1)S(1)} %copy.72), kind=kLoop, calls=%fused_computation.25 | loop fusion | flops 1572864 | bytes 3158016 | tf_op jit(solution)/shard_map/jit(_where)/select_n | solution.py:56
  98.2 0.0 copy-start.3
  98.2 0.0 copy-start.4
  98.2 0.0 copy-done.5
  98.2 0.7 convolution_convert_fusion.1
  99.0 0.8 copy-done.4
  99.8 0.7 convolution_convert_fusion
  100.5 0.0 copy-start.10
  100.6 2.8 fusion.15
  103.4 0.0 copy-done.10
  103.4 0.8 fusion.1
  104.2 0.0 copy-done.3
  104.2 2.7 fusion.5
  106.9 2.1 convolution_add_fusion
  108.9 2.7 reshape.213
  111.7 8.2 %pad_maximum_fusion = f32[2048,1024]{1,0:T(8,128)} fusion(f32[2048,512]{1,0:T(8,128)} %fusion.15, f32[2048,512]{1,0:T(8,128)} %fusion.5), kind=kLoop, calls=%fused_computation.6 | loop fusion | flops 2097152 | bytes 16777216 | tf_op jit(solution)/shard_map/concatenate | solution.py:107
  119.8 23.6 %scatter_custom_fusion = f32[2048,128]{1,0:T(8,128)} fusion(s32[4096]{0:T(1024)S(1)} %bitcast.43, f32[4096,128]{1,0:T(8,128)} %reshape.213, f32[]{:T(128)} %constant.31.clone.1), kind=kCustom, calls=%fused_computation.32 | custom fusion | flops 524288 | bytes 1049088 | tf_op jit(solution)/shard_map/scatter-add | solution.py:97
  143.5 0.0 all-reduce.3.cloned.1.call-update
  143.5 0.2 all-gather.2.cloned.1.call-start
  143.7 160.4 %all-reduce.3.cloned.1.call-done = (f32[2048,128]{1,0:T(8,128)}, f32[2048,1024]{1,0:T(8,128)}) async-done(((f32[2048,128]{1,0:T(8,128)}, f32[2048,1024]{1,0:T(8,128)}), (f32[2048,128]{1,0:T(8,128)}, f32[2048,1024]{1,0:T(8,128)})) %all-reduce.3.cloned.1.call-update) | async-done | bytes 9437200 | tf_op jit(solution)/shard_map/psum | solution.py:106
  304.2 1.5 fusion.18
  305.7 0.0 all-gather.2.cloned.1.call-update
  305.7 0.1 copy.78
  305.8 0.1 reshape.172
  306.0 23.9 %scatter_custom_fusion.1 = f32[3072,128]{1,0:T(8,128)} fusion(s32[4096]{0:T(1024)S(1)} %bitcast.44, f32[4096,128]{1,0:T(8,128)} %reshape.213, f32[]{:T(128)} %constant.31.clone.1), kind=kCustom, calls=%fused_computation.28 | custom fusion | flops 524288 | bytes 1573376 | tf_op jit(solution)/shard_map/scatter-add | solution.py:78
  329.8 2.4 convert_element_type.39
  332.2 7.2 %all-to-all-start.2 = ((bf16[128,24,128]{2,1,0:T(8,128)(2,1)}), bf16[128,24,128]{2,1,0:T(8,128)(2,1)}, u32[]{:S(2)}, u32[]{:S(2)}) async-start(bf16[128,24,128]{2,1,0:T(8,128)(2,1)} %bitcast.8), calls=%async_computation.2 | async-start | bytes 1572864 | tf_op jit(solution)/shard_map/all_to_all | solution.py:80
  339.4 0.0 copy-start.2
  339.4 2.1 convert_reduce_fusion
  341.5 67.6 %psum.22 = f32[2048]{0:T(1024)S(1)} all-reduce(f32[2048]{0:T(1024)S(1)} %convert_reduce_fusion), channel_id=1, replica_groups=mesh['dev'=128] {'dev'}, use_global_device_ids=true, to_apply=%region_3.4 | all-reduce | flops 2048 | bytes 16384 | tf_op jit(solution)/shard_map/psum | solution.py:106
  409.1 0.6 broadcast_multiply_fusion.1
  409.7 0.0 all-to-all-done.2
  409.7 18.3 %scatter_custom_fusion.2 = f32[2048,128]{1,0:T(8,128)} fusion(s32[3072]{0:T(1024)S(1)} %bitcast.42, bf16[3072,128]{1,0:T(8,128)(2,1)} %bitcast.10, f32[]{:T(128)} %constant.31.clone.1), kind=kCustom, calls=%fused_computation.14 | custom fusion | flops 786432 | bytes 1835012 | tf_op jit(solution)/shard_map/scatter-add | solution.py:90
  428.0 4.0 divide_subtract_fusion
  432.0 0.0 copy-done.6
  432.0 1.0 broadcast_multiply_fusion
  433.1 4.6 %copy.100 = bf16[2048,1024]{1,0:T(8,128)(2,1)} copy(bf16[2048,1024]{1,0:T(8,128)(2,1)} %all-gather.2.cloned.1.call-done) | data formatting | bytes 8388608
  (20 shorter events, 0.1 us)
Async XLA Ops:
  7.2 91.8 %copy-start = (bf16[512,2048]{1,0:T(8,128)(2,1)S(1)}, bf16[512,2048]{1,0:T(8,128)(2,1)}, u32[]{:S(2)}) copy-start(bf16[512,2048]{1,0:T(8,128)(2,1)} %param.20) | copy-start | bytes 6291460
  7.2 17.0 %copy-start.1 = (bf16[2048,128]{1,0:T(8,128)(2,1)S(1)}, bf16[2048,128]{1,0:T(8,128)(2,1)}, u32[]{:S(2)}) copy-start(bf16[2048,128]{1,0:T(8,128)(2,1)} %param.15) | copy-start | bytes 1572868
  8.8 30.5 %all-to-all-start = ((s32[1,128,24]{2,0,1:T(1,128)}), s32[1,128,24]{2,0,1:T(1,128)S(1)}, u32[]{:S(2)}, u32[]{:S(2)}) async-start(s32[1,128,24]{2,0,1:T(1,128)} %copy.76), calls=%async_computation | async-start | bytes 131072 | tf_op jit(solution)/shard_map/all_to_all | solution.py:47
  51.7 26.0 %all-to-all-start.1 = ((bf16[128,24,128]{2,1,0:T(8,128)(2,1)}), bf16[128,24,128]{2,1,0:T(8,128)(2,1)S(1)}, u32[]{:S(2)}, u32[]{:S(2)}) async-start(bf16[128,24,128]{2,1,0:T(8,128)(2,1)} %select_convert_fusion), calls=%async_computation.1 | async-start | bytes 1572864 | tf_op jit(solution)/shard_map/all_to_all | solution.py:50
  61.4 242.7 %all-reduce.3.cloned.1.call-start = ((), (), s32[]{:S(2)}) async-start(), calls=%async_computation.4 | async-start | bytes 18874368 | tf_op jit(solution)/shard_map/psum | solution.py:106
  92.7 5.6 %copy-start.5 = (bf16[2048,512]{1,0:T(8,128)(2,1)S(1)}, bf16[2048,512]{1,0:T(8,128)(2,1)}, u32[]{:S(2)}) copy-start(bf16[2048,512]{1,0:T(8,128)(2,1)} %param.19) | copy-start | bytes 6291460
  98.2 6.0 %copy-start.3 = (bf16[256,16,128]{2,1,0:T(8,128)(2,1)}, bf16[256,16,128]{2,1,0:T(8,128)(2,1)S(1)}, u32[]{:S(2)}) copy-start(bf16[256,16,128]{2,1,0:T(8,128)(2,1)S(1)} %select_select_fusion) | copy-start | bytes 3145732
  98.2 1.6 copy-start.4
  100.5 2.8 copy-start.10
  143.5 160.7 %copy-start.7 = (f32[16,1024]{1,0:T(8,128)S(1)}, f32[16,1024]{1,0:T(8,128)}, u32[]{:S(2)}) copy-start(f32[16,1024]{1,0:T(8,128)} %param.22) | copy-start | bytes 196612
  143.5 160.7 %copy-start.8 = (f32[16,1024]{1,0:T(8,128)S(1)}, f32[16,1024]{1,0:T(8,128)}, u32[]{:S(2)}) copy-start(f32[16,1024]{1,0:T(8,128)} %param.23) | copy-start | bytes 196612
  143.5 160.7 %copy-start.9 = (f32[16,1024]{1,0:T(8,128)S(1)}, f32[16,1024]{1,0:T(8,128)}, u32[]{:S(2)}) copy-start(f32[16,1024]{1,0:T(8,128)} %param.24) | copy-start | bytes 196612
  143.5 289.6 %all-gather.2.cloned.1.call-start = ((), (), s32[]{:S(2)}) async-start(), calls=%async_computation.3 | async-start | bytes 4227072 | tf_op jit(solution)/shard_map/all_gather | solution.py:115
  332.2 77.5 %all-to-all-start.2 = ((bf16[128,24,128]{2,1,0:T(8,128)(2,1)}), bf16[128,24,128]{2,1,0:T(8,128)(2,1)}, u32[]{:S(2)}, u32[]{:S(2)}) async-start(bf16[128,24,128]{2,1,0:T(8,128)(2,1)} %bitcast.8), calls=%async_computation.2 | async-start | bytes 1572864 | tf_op jit(solution)/shard_map/all_to_all | solution.py:80
  339.4 88.6 %copy-start.2 = (f32[2048,128]{1,0:T(8,128)S(1)}, f32[2048,128]{1,0:T(8,128)}, u32[]{:S(2)}) copy-start(f32[2048,128]{1,0:T(8,128)} %param.16) | copy-start | bytes 3145732
  428.0 4.0 copy-start.6
Sparse Core Ops, SparseCore 0:
  143.6 160.5 all-reduce.2
  307.3 70.9 all-gather.1
where the time goes:
time: 445 us
  waiting for transfers between devices  177 us (40%)
  other arithmetic  96.2 us (22%)
  blocking collectives  67.6 us (15%)
  local copies, waits for them, and re-layouts  51.3 us (12%)
  starting transfers between devices  28.7 us (6%)
  between operations  14.3 us (3%)
  matrix products  9.81 us (2%)
    psum x1, waiting for transfers between devices, body(): lax.psum((jnp.concatenate([down_part, up_part], axis=1), hot_part, bias_p...  160 us
    psum x1, blocking collectives, body(): lax.psum((jnp.concatenate([down_part, up_part], axis=1), hot_part, bias_p...  67.6 us
    scatter-add x1, other arithmetic, body(): cold_part = jnp.zeros((devices * capacity, emb_width), jnp.float32).at[co...  23.9 us
    scatter-add x1, other arithmetic, body(): jnp.zeros((hot_rows, emb_width), jnp.float32).at[hot_target]  23.6 us
    scatter-add x1, other arithmetic, body(): cold_sum = jnp.zeros((slab_rows, emb_width), jnp.float32).at[request_flat...  18.3 us
    all_to_all x1, waiting for transfers between devices, body(): lax.all_to_all(picked.reshape(devices, capacity, emb_width), 'dev', split...  16.1 us
    gather x1, local copies, waits for them, and re-layouts, body(): jnp.take(hot_table, hot_ids, axis=0)  15 us
    gather x1, local copies, waits for them, and re-layouts, body(): jnp.take(fetched_flat, cold_pos, axis=0)  15 us
  transfers between devices with their start and end apart: 5, of which 2 were waited for; matrix products, arithmetic and copies ran while one was open for 16% of the time, Pallas kernels for 0%

commit v1 on v0

--- a/solution.py
+++ b/solution.py
@@ -1,7 +1,11 @@
 import jax
 import jax.numpy as jnp
 from jax import lax
+from jax.experimental import pallas as pl
+from jax.experimental.pallas import tpu as pltpu
 from jax.sharding import PartitionSpec as P
+
+MESH = pl.DeviceIdType.MESH
 
 first_decay = 0.9
 second_decay = 0.999
@@ -18,6 +22,167 @@
         jnp.sqrt(moment_two / second_fix) + adam_epsilon
     )
     return (params, moment_one, moment_two)
+
+CUTS = ((0, 384), (384, 768), (768, 1280))
+ORDERS = ((0, 1, 2), (1, 2, 0), (2, 0, 1))
+
+
+def coords_of(me):
+    return [me // 32, lax.rem(me // 8, 4), lax.rem(me // 2, 4)], lax.rem(me, 2)
+
+
+def device_of(place, core):
+    return place[0] * 32 + place[1] * 8 + place[2] * 2 + core
+
+
+def moved(place, axis, step):
+    return [lax.rem(p + step, 4) if a == axis else p for a, p in enumerate(place)]
+
+
+def reduce_kernel(part, master, m_in, v_in, out, master_out, m_out, v_out, *rest):
+    first, sums0, got1, sums1, got2, sums2, got3 = (rest[3 * i : 3 * i + 3] for i in range(7))
+    total, send_sem, recv_sem = rest[21:]
+    place, core = coords_of(lax.axis_index("dev"))
+    barrier = pltpu.get_barrier_semaphore()
+    others = [device_of(place, 1 - core)]
+    others += [device_of(moved(place, a, s), core) for a in range(3) for s in (1, 2, 3)]
+    for other in others:
+        pl.semaphore_signal(barrier, inc=1, device_id=(other,), device_id_type=MESH)
+    pl.semaphore_wait(barrier, len(others))
+    started = []
+
+    def send(src, dst, color, phase, slot, other):
+        copy = pltpu.make_async_remote_copy(
+            src_ref=src,
+            dst_ref=dst,
+            send_sem=send_sem.at[color, phase, slot],
+            recv_sem=recv_sem.at[color, phase, slot],
+            device_id=(other,),
+            device_id_type=MESH,
+        )
+        copy.start()
+        started.append(copy)
+        return copy
+
+    waiting = {}
+    for k, (low, high) in enumerate(CUTS):
+        waiting[k] = [
+            send(
+                part.at[:, :, :, 1 - core, :, low:high],
+                first[k],
+                k,
+                0,
+                0,
+                device_of(place, 1 - core),
+            )
+        ]
+    for phase in range(4):
+        for k, (low, high) in enumerate(CUTS):
+            order = ORDERS[k]
+            for copy in waiting[k]:
+                copy.wait_recv()
+            if phase == 0:
+
+                def add_first(i, carry):
+                    a = [i // 16, lax.rem(i // 4, 4), lax.rem(i, 4)]
+                    zxy = [a[order.index(axis)] for axis in range(3)]
+                    mine = part[zxy[0], zxy[1], zxy[2], core, :, low:high].astype(jnp.float32)
+                    other = first[k][zxy[0], zxy[1], zxy[2]].astype(jnp.float32)
+                    sums0[k][a[0], a[1], a[2]] = (mine + other).astype(jnp.bfloat16)
+                    return carry
+
+                lax.fori_loop(0, 64, add_first, 0)
+            elif phase < 3:
+                source = (sums0, sums1)[phase - 1][k].at[place[order[phase - 1]]]
+                got = (got1, got2)[phase - 1][k]
+                into = (sums1, sums2)[phase - 1][k]
+
+                def add_more(i, carry):
+                    at = (i // 4, lax.rem(i, 4)) if phase == 1 else (i,)
+                    acc = source[at].astype(jnp.float32)
+                    for slot in range(3):
+                        acc = acc + got[(slot,) + at].astype(jnp.float32)
+                    into[at] = acc.astype(jnp.bfloat16)
+                    return carry
+
+                lax.fori_loop(0, 16 if phase == 1 else 4, add_more, 0)
+            else:
+                acc = sums2[k][place[order[2]]].astype(jnp.float32)
+                for slot in range(3):
+                    acc = acc + got3[k][slot].astype(jnp.float32)
+                total[:, low:high] = acc
+            if phase < 3:
+                axis = order[phase]
+                source = (sums0, sums1, sums2)[phase][k]
+                into = (got1, got2, got3)[phase][k]
+                waiting[k] = [
+                    send(
+                        source.at[moved(place, axis, s)[axis]],
+                        into.at[s - 1],
+                        k,
+                        1 + phase,
+                        s - 1,
+                        device_of(moved(place, axis, s), core),
+                    )
+                    for s in (1, 2, 3)
+                ]
+    scale = 1.0 / 128.0
+    new, m_new, v_new = adam_update(master[...], m_in[...], v_in[...], total[:, :1024] * scale)
+    master_out[...] = new
+    m_out[...] = m_new
+    v_out[...] = v_new
+    out[place[0], place[1], place[2], core, :, :1024] = new.astype(jnp.bfloat16)
+    out[place[0], place[1], place[2], core, :, 1024:] = (total[:, 1024:] * scale).astype(
+        jnp.bfloat16
+    )
+    for phase in range(4):
+        for k, (low, high) in enumerate(CUTS):
+            order = ORDERS[k]
+            for copy in waiting[k] if phase else []:
+                copy.wait_recv()
+            spread = order[3 - phase :]
+            at = tuple(slice(None) if a in spread else place[a] for a in range(3))
+            block = out.at[at + (core, slice(None), slice(low, high))]
+            if phase < 3:
+                axis = order[2 - phase]
+                waiting[k] = [
+                    send(
+                        block, block, k, 4 + phase, s - 1, device_of(moved(place, axis, s), core)
+                    )
+                    for s in (1, 2, 3)
+                ]
+            else:
+                waiting[k] = [send(block, block, k, 7, 0, device_of(place, 1 - core))]
+    for k in range(3):
+        for copy in waiting[k]:
+            copy.wait_recv()
+    for copy in started:
+        copy.wait_send()
+
+
+def reduce_all(part, master, m_in, v_in):
+    widths = [high - low for low, high in CUTS]
+    shapes = ((4, 4, 4), (4, 4, 4), (3, 4, 4), (4, 4), (3, 4), (4,), (3,))
+    small = jax.ShapeDtypeStruct(master.shape, jnp.float32)
+    vmem = pl.BlockSpec(memory_space=pltpu.VMEM)
+    return pl.pallas_call(
+        reduce_kernel,
+        out_shape=(jax.ShapeDtypeStruct(part.shape, jnp.bfloat16), small, small, small),
+        in_specs=[vmem] * 4,
+        out_specs=(vmem,) * 4,
+        scratch_shapes=[
+            pltpu.VMEM(shape + (16, width), jnp.bfloat16) for shape in shapes for width in widths
+        ]
+        + [
+            pltpu.VMEM((16, part.shape[-1]), jnp.float32),
+            pltpu.SemaphoreType.DMA((3, 8, 3)),
+            pltpu.SemaphoreType.DMA((3, 8, 3)),
+        ],
+        compiler_params=pltpu.CompilerParams(
+            collective_id=0, has_side_effects=True, vmem_limit_bytes=48 * 2**20
+        ),
+        name="reduce_all",
+    )(part, master, m_in, v_in)
 
 
 def body(
@@ -103,19 +268,19 @@
     up_part = lax.dot_general(
         grad_mix, latent, (((0,), (0,)), ((), ())), preferred_element_type=jnp.float32
     )
-    dense_total, hot_sum, bias_sum = lax.psum(
-        (jnp.concatenate([down_part, up_part], axis=1), hot_part, bias_part), "dev"
-    )
-    dense_own = lax.dynamic_slice_in_dim(
-        dense_total, lax.axis_index("dev") * shard_rows, shard_rows, 0
-    )
-    master_new, dense_m_new, dense_v_new = adam_update(
-        dense_master, dense_m, dense_v, dense_own * scale_mean
-    )
-    new_weights = lax.all_gather(master_new.astype(jnp.bfloat16), "dev", axis=0, tiled=True)
+    column = jnp.pad(bias_part[:, None], ((0, 0), (0, emb_width - 1)))
+    part = jnp.concatenate([down_part, up_part, hot_part, column], axis=1).astype(jnp.bfloat16)
+    gathered, master_new, dense_m_new, dense_v_new = reduce_all(
+        part.reshape(4, 4, 4, 2, shard_rows, part.shape[1]), dense_master, dense_m, dense_v
+    )
+    flat = gathered.reshape(part.shape)
+    dense_cols = dense_master.shape[1]
+    hot_grad = flat[:, dense_cols : dense_cols + emb_width].astype(jnp.float32)
+    bias_grad = flat[:, dense_cols + emb_width].astype(jnp.float32)
+    new_weights = flat[:, :dense_cols]
     return (
-        hot_sum * scale_mean,
-        bias_sum * scale_mean,
+        hot_grad,
+        bias_grad,
         cold_new,
         cold_m_new,
         cold_v_new,

time: 445 us -> 264 us (0.59)
  waiting for transfers between devices: 177 us -> 16.2 us
  blocking collectives: 67.6 us -> 0 us
  Pallas kernels: 0 us -> 62.6 us
  between operations: 14.3 us -> 0.93 us
  other arithmetic: 96.2 us -> 89.5 us
  local copies, waits for them, and re-layouts: 51.3 us -> 56.7 us
    psum x1 -> x0, waiting for transfers between devices: 160 us -> none  [body(): lax.psum((jnp.concatenate([down_part, up_part], axis=1), hot_part, bias_p...]
    psum x1 -> x0, blocking collectives: 67.6 us -> none  [body(): lax.psum((jnp.concatenate([down_part, up_part], axis=1), hot_part, bias_p...]
    pallas_call x0 -> x1, Pallas kernels: none -> 62.6 us  [reduce_all(): pl.pallas_call(reduce_kernel, out_shape=(jax.ShapeDtypeStruct(part.shape,...]
  transfers between devices with their start and end apart: 5 -> 3, of which waited for: 2 -> 1; matrix products, arithmetic and copies ran while one was open for 16% -> 11% of each run, Pallas kernels for 0% -> 24%
where the time goes in v1:
time: 264 us; the launch traced here: 263 us
  other arithmetic  89.5 us (34%)
  Pallas kernels  62.6 us (24%)
  local copies, waits for them, and re-layouts  56.7 us (21%)
  starting transfers between devices  26.9 us (10%)
  waiting for transfers between devices  16.2 us (6%)
  matrix products  10.6 us (4%)
    pallas_call x1, Pallas kernels, reduce_all(): pl.pallas_call(reduce_kernel, out_shape=(jax.ShapeDtypeStruct(part.shape,...  62.6 us
    scatter-add x1, other arithmetic, body(): cold_part = jnp.zeros((devices * capacity, emb_width), jnp.float32).at[co...  23.9 us
    scatter-add x1, other arithmetic, body(): jnp.zeros((hot_rows, emb_width), jnp.float32).at[hot_target]  23.1 us
    scatter-add x1, other arithmetic, body(): cold_sum = jnp.zeros((slab_rows, emb_width), jnp.float32).at[request_flat...  18.3 us
    all_to_all x1, waiting for transfers between devices, body(): lax.all_to_all(picked.reshape(devices, capacity, emb_width), 'dev', split...  16.2 us
    gather x1, local copies, waits for them, and re-layouts, body(): jnp.take(hot_table, hot_ids, axis=0)  15 us
    gather x1, local copies, waits for them, and re-layouts, body(): jnp.take(fetched_flat, cold_pos, axis=0)  15 us
    all_to_all x1, starting transfers between devices, body(): lax.all_to_all(fetch_rows, 'dev', split_axis=1, concat_axis=0, tiled=True)  11.5 us
  transfers between devices with their start and end apart: 3, of which 1 were waited for; matrix products, arithmetic and copies ran while one was open for 11% of the time, Pallas kernels for 24%

profile of v1, /device:TPU:1, one launch (start us, length us, event | category | flops | bytes accessed | tf_op | source)
XLA Modules:
  0.0 263.5 jit_solution(14401230268023215621)
XLA Ops:
  0.6 0.0 copy-start
  0.7 1.6 copy.43
  2.3 11.5 %all-to-all-start = ((s32[1,128,24]{2,0,1:T(1,128)}), s32[1,128,24]{2,0,1:T(1,128)S(1)}, u32[]{:S(2)}, u32[]{:S(2)}) async-start(s32[1,128,24]{2,0,1:T(1,128)} %copy.43), calls=%async_computation | async-start | bytes 131072 | tf_op jit(solution)/shard_map/all_to_all | solution.py:212
  13.8 0.7 compare_and_fusion.1
  14.5 0.7 broadcast_select_fusion
  15.2 0.7 broadcast_select_fusion.1
  15.9 0.1 copy.46
  16.0 0.1 reshape.184
  16.2 0.1 copy.41
  16.3 0.1 reshape.195
  16.4 0.1 copy.44
  16.5 0.1 reshape.211
  16.6 0.7 broadcast_compare_fusion
  17.3 0.1 copy.39
  17.5 0.1 copy.42
  17.6 0.1 copy.40
  17.7 0.1 copy.48
  17.8 0.1 reshape.187
  18.0 15.0 %gather_fusion = bf16[4096,128]{1,0:T(8,128)(2,1)} fusion(bf16[2048,128]{1,0:T(8,128)(2,1)S(1)} %copy-done.4, s32[4096]{0:T(1024)S(1)} %broadcast_clamp_fusion.1), kind=kCustom, calls=%fused_computation | custom fusion | bytes 2113536 | tf_op jit(solution)/shard_map/jit(_take)/gather | solution.py:223
  33.0 0.0 all-to-all-done
  33.0 0.5 broadcast.126
  33.5 0.8 reduce.7
  34.4 0.1 reshape.182
  34.5 9.5 %gather_fusion.1 = bf16[3072,128]{1,0:T(8,128)(2,1)S(1)} fusion(f32[2048,128]{1,0:T(8,128)} %param.16, s32[3072]{0:T(1024)S(1)} %broadcast_clamp_fusion.2), kind=kCustom, calls=%fused_computation.1 | custom fusion | bytes 1585152 | tf_op jit(solution)/shard_map/jit(_take)/gather | solution.py:214
  44.0 1.3 select_convert_fusion
  45.4 9.8 %all-to-all-start.1 = ((bf16[128,24,128]{2,1,0:T(8,128)(2,1)}), bf16[128,24,128]{2,1,0:T(8,128)(2,1)S(1)}, u32[]{:S(2)}, u32[]{:S(2)}) async-start(bf16[128,24,128]{2,1,0:T(8,128)(2,1)} %select_convert_fusion), calls=%async_computation.1 | async-start | bytes 1572864 | tf_op jit(solution)/shard_map/all_to_all | solution.py:215
  55.2 16.2 %all-to-all-done.1 = bf16[128,24,128]{2,1,0:T(8,128)(2,1)S(1)} async-done(((bf16[128,24,128]{2,1,0:T(8,128)(2,1)}), bf16[128,24,128]{2,1,0:T(8,128)(2,1)S(1)}, u32[]{:S(2)}, u32[]{:S(2)}) %all-to-all-start.1) | async-done | bytes 786464 | tf_op jit(solution)/shard_map/all_to_all | solution.py:215
  71.3 15.0 %gather_fusion.2 = bf16[4096,128]{1,0:T(8,128)(2,1)} fusion(bf16[3072,128]{1,0:T(8,128)(2,1)S(1)} %bitcast.47, s32[4096]{0:T(1024)S(1)} %broadcast_clamp_fusion), kind=kCustom, calls=%fused_computation.2 | custom fusion | bytes 2113536 | tf_op jit(solution)/shard_map/jit(_take)/gather | solution.py:224
  86.4 5.5 %select_select_fusion = bf16[256,16,128]{2,1,0:T(8,128)(2,1)S(1)} fusion(bf16[256,16,128]{2,1,0:T(8,128)(2,1)} %bitcast.55, bf16[256,16,128]{2,1,0:T(8,128)(2,1)} %bitcast.54, pred[256,16]{1,0:T(8,128)(4,1)S(1)} %copy.42, pred[256,16]{1,0:T(8,128)(4,1)S(1)} %copy.40, pred[256,16]{1,0:T(8,128)(4,1)S(1)} %copy.39), kind=kLoop, calls=%fused_computation.26 | loop fusion | flops 1572864 | bytes 3158016 | tf_op jit(solution)/shard_map/jit(_where)/select_n | solution.py:221
  91.8 0.0 copy-start.9
  91.8 1.2 copy.62
  93.1 0.5 fusion.13
  93.6 0.2 copy-done.9
  93.8 1.4 convolution_convert_fusion.2
  95.2 0.7 convolution_convert_fusion.3
  96.0 1.1 broadcast_in_dim.66
  97.1 2.3 copy.45
  99.4 3.5 %convolution_convert_fusion = bf16[2048,512]{1,0:T(8,128)(2,1)} fusion(bf16[256,512]{1,0:T(8,128)(2,1)} %convolution_convert_fusion.2, bf16[256,2048]{1,0:T(8,128)(2,1)} %param.14, bf16[32,8,16,128]{3,2,1,0:T(8,128)(2,1)S(1)} %bitcast.52), kind=kOutput, calls=%fused_computation.7 | convolution fusion | flops 540016640 | bytes 4456448 | tf_op jit(solution)/shard_map/dot_general | solution.py:268
  102.9 0.0 copy-start.8
  103.0 0.8 fusion.1
  103.7 0.0 copy-start.10
  103.7 0.4 copy-done.8
  104.2 2.1 convolution_convert_fusion.1
  106.3 2.1 convolution_add_fusion
  108.3 2.7 %reshape.229 = f32[4096,128]{1,0:T(8,128)} reshape(f32[256,2048]{1,0:T(8,128)} %convolution_add_fusion) | data formatting | bytes 4194304 | tf_op jit(solution)/shard_map/reshape | solution.py:238
  111.1 23.1 %scatter_custom_fusion = f32[2048,128]{1,0:T(8,128)S(1)} fusion(s32[4096]{0:T(1024)S(1)} %bitcast.65, f32[4096,128]{1,0:T(8,128)} %reshape.229, f32[]{:T(128)} %constant.39.clone.1), kind=kCustom, calls=%fused_computation.32 | custom fusion | flops 524288 | bytes 1049088 | tf_op jit(solution)/shard_map/scatter-add | solution.py:262
  134.2 23.9 %scatter_custom_fusion.1 = f32[3072,128]{1,0:T(8,128)} fusion(s32[4096]{0:T(1024)S(1)} %bitcast.66, f32[4096,128]{1,0:T(8,128)} %reshape.229, f32[]{:T(128)} %constant.39.clone.1), kind=kCustom, calls=%fused_computation.28 | custom fusion | flops 524288 | bytes 1573376 | tf_op jit(solution)/shard_map/scatter-add | solution.py:243
  158.0 2.4 convert_element_type.52
  160.4 0.8 convert.22
  161.2 5.7 %all-to-all-start.2 = ((bf16[128,24,128]{2,1,0:T(8,128)(2,1)}), bf16[128,24,128]{2,1,0:T(8,128)(2,1)}, u32[]{:S(2)}, u32[]{:S(2)}) async-start(bf16[128,24,128]{2,1,0:T(8,128)(2,1)} %bitcast.58), calls=%async_computation.2 | async-start | bytes 1572864 | tf_op jit(solution)/shard_map/all_to_all | solution.py:245
  166.9 1.1 pad.5.clone
  168.1 0.0 copy-start.1
  168.1 0.0 copy-start.2
  168.1 0.0 copy-start.3
  168.1 4.2 %pad_maximum_fusion.part = bf16[4,4,4,2,16,1280]{5,4,3,2,1,0:T(8,128)(2,1)} fusion(bf16[4,4,4,2,16,128]{5,4,3,2,1,0:T(8,128)(2,1)S(1)} %bitcast.61, bf16[4,4,4,2,16,128]{5,4,3,2,1,0:T(8,128)(2,1)S(1)} %bitcast.60, bf16[4,4,4,2,16,512]{5,4,3,2,1,0:T(8,128)(2,1)} %bitcast.53, bf16[4,4,4,2,16,512]{5,4,3,2,1,0:T(8,128)(2,1)} %convolution_convert_fusion.1), kind=kLoop, calls=%fused_computation.6 | loop fusion | flops 20971520 | bytes 10485760 | tf_op jit(solution)/shard_map/concatenate | solution.py:272
  172.4 62.6 %reduce_all.1 = (bf16[4,4,4,2,16,1280]{5,4,3,2,1,0:T(8,128)(2,1)S(1)}, f32[16,1024]{1,0:T(8,128)S(1)}, f32[16,1024]{1,0:T(8,128)S(1)}, f32[16,1024]{1,0:T(8,128)S(1)}) custom-call(bf16[4,4,4,2,16,1280]{5,4,3,2,1,0:T(8,128)(2,1)} %pad_maximum_fusion.part, f32[16,1024]{1,0:T(8,128)S(1)} %copy-done.1, f32[16,1024]{1,0:T(8,128)S(1)} %copy-done.2, ...), custom_call_target="tpu_custom_call" | custom-call | tf_op jit(solution)/shard_map/reduce_all/pallas_call | solution.py:168
  234.9 2.6 slice.20
  237.5 0.8 convert_reduce_fusion
  238.3 1.0 slice_convert_fusion
  239.4 18.3 %scatter_custom_fusion.2 = f32[2048,128]{1,0:T(8,128)} fusion(s32[3072]{0:T(1024)S(1)} %bitcast.64, bf16[3072,128]{1,0:T(8,128)(2,1)} %bitcast.19, f32[]{:T(128)} %constant.39.clone.1), kind=kCustom, calls=%fused_computation.15 | custom fusion | flops 786432 | bytes 1835012 | tf_op jit(solution)/shard_map/scatter-add | solution.py:255
  257.7 3.9 %divide_subtract_fusion = (f32[2048,128]{1,0:T(8,128)}, f32[2048,128]{1,0:T(8,128)}, f32[2048,128]{1,0:T(8,128)}) fusion(f32[2048,128]{1,0:T(8,128)S(1)} %copy-done.5, f32[2048,128]{1,0:T(8,128)} %scatter_custom_fusion.2, f32[2048,128]{1,0:T(8,128)} %param.17, f32[2048,128]{1,0:T(8,128)} %param.18), kind=kLoop, calls=%fused_computation.23 | loop fusion | flops 3407872 | bytes 7340032 | tf_op jit(solution)/shard_map/sub | solution.py:21
  261.6 0.6 copy.66
  262.2 0.6 copy.67
  262.8 0.6 copy.68
  (27 shorter events, 0.1 us)
Async XLA Ops:
  0.6 94.6 %copy-start = (bf16[512,2048]{1,0:T(8,128)(2,1)S(1)}, bf16[512,2048]{1,0:T(8,128)(2,1)}, u32[]{:S(2)}) copy-start(bf16[512,2048]{1,0:T(8,128)(2,1)} %param.20) | copy-start | bytes 6291460
  0.7 17.3 %copy-start.4 = (bf16[2048,128]{1,0:T(8,128)(2,1)S(1)}, bf16[2048,128]{1,0:T(8,128)(2,1)}, u32[]{:S(2)}) copy-start(bf16[2048,128]{1,0:T(8,128)(2,1)} %param.15) | copy-start | bytes 1572868
  2.3 30.7 %all-to-all-start = ((s32[1,128,24]{2,0,1:T(1,128)}), s32[1,128,24]{2,0,1:T(1,128)S(1)}, u32[]{:S(2)}, u32[]{:S(2)}) async-start(s32[1,128,24]{2,0,1:T(1,128)} %copy.43), calls=%async_computation | async-start | bytes 131072 | tf_op jit(solution)/shard_map/all_to_all | solution.py:212
  45.4 26.0 %all-to-all-start.1 = ((bf16[128,24,128]{2,1,0:T(8,128)(2,1)}), bf16[128,24,128]{2,1,0:T(8,128)(2,1)S(1)}, u32[]{:S(2)}, u32[]{:S(2)}) async-start(bf16[128,24,128]{2,1,0:T(8,128)(2,1)} %select_convert_fusion), calls=%async_computation.1 | async-start | bytes 1572864 | tf_op jit(solution)/shard_map/all_to_all | solution.py:215
  86.4 6.7 %copy-start.6 = (bf16[256,2048]{1,0:T(8,128)(2,1)S(1)}, bf16[256,2048]{1,0:T(8,128)(2,1)}, u32[]{:S(2)}) copy-start(bf16[256,2048]{1,0:T(8,128)(2,1)} %param.14) | copy-start | bytes 3145732
  91.8 2.0 copy-start.9
  99.4 3.6 %copy-start.7 = (bf16[256,2048]{1,0:T(8,128)(2,1)S(1)}, bf16[256,2048]{1,0:T(8,128)(2,1)}, u32[]{:S(2)}) copy-start(bf16[256,2048]{1,0:T(8,128)(2,1)} %param.14) | copy-start | bytes 3145732
  99.4 3.6 %copy-start.12 = (bf16[256,512]{1,0:T(8,128)(2,1)S(1)}, bf16[256,512]{1,0:T(8,128)(2,1)}, u32[]{:S(2)}) copy-start(bf16[256,512]{1,0:T(8,128)(2,1)} %convolution_convert_fusion.2) | copy-start | bytes 786436
  99.4 3.6 %copy-start.13 = (f32[2048]{0:T(1024)S(1)}, f32[2048]{0:T(1024)}, u32[]{:S(2)}) copy-start(f32[2048]{0:T(1024)} %param.21) | copy-start | bytes 24580
  102.9 1.2 copy-start.8
  103.7 2.5 copy-start.10
  161.2 6.9 %copy-start.11 = (bf16[2048,128]{1,0:T(8,128)(2,1)S(1)}, bf16[2048,128]{1,0:T(8,128)(2,1)}, u32[]{:S(2)}) copy-start(bf16[2048,128]{1,0:T(8,128)(2,1)} %convert.22) | copy-start | bytes 1572868
  161.2 78.2 %all-to-all-start.2 = ((bf16[128,24,128]{2,1,0:T(8,128)(2,1)}), bf16[128,24,128]{2,1,0:T(8,128)(2,1)}, u32[]{:S(2)}, u32[]{:S(2)}) async-start(bf16[128,24,128]{2,1,0:T(8,128)(2,1)} %bitcast.58), calls=%async_computation.2 | async-start | bytes 1572864 | tf_op jit(solution)/shard_map/all_to_all | solution.py:245
  168.1 4.3 %copy-start.1 = (f32[16,1024]{1,0:T(8,128)S(1)}, f32[16,1024]{1,0:T(8,128)}, u32[]{:S(2)}) copy-start(f32[16,1024]{1,0:T(8,128)} %master.1) | copy-start | bytes 196612
  168.1 4.2 %copy-start.2 = (f32[16,1024]{1,0:T(8,128)S(1)}, f32[16,1024]{1,0:T(8,128)}, u32[]{:S(2)}) copy-start(f32[16,1024]{1,0:T(8,128)} %m_in.1) | copy-start | bytes 196612
  168.1 4.2 %copy-start.3 = (f32[16,1024]{1,0:T(8,128)S(1)}, f32[16,1024]{1,0:T(8,128)}, u32[]{:S(2)}) copy-start(f32[16,1024]{1,0:T(8,128)} %v_in.1) | copy-start | bytes 196612
  237.5 20.1 %copy-start.5 = (f32[2048,128]{1,0:T(8,128)S(1)}, f32[2048,128]{1,0:T(8,128)}, u32[]{:S(2)}) copy-start(f32[2048,128]{1,0:T(8,128)} %param.16) | copy-start | bytes 3145732

commit v2 on v1

--- a/solution.py
+++ b/solution.py
@@ -184,6 +184,257 @@
         name="reduce_all",
     )(part, master, m_in, v_in)
 
+def peer_of(place, core, step):
+    hops = (step // 32, lax.rem(step // 8, 4), lax.rem(step // 2, 4))
+    there = [lax.rem(p + h, 4) for p, h in zip(place, hops)]
+    return device_of(there, lax.rem(core + step, 2))
+
+
+def fetch_kernel(
+    lists, table, arrived, got, asked, picked, block, list_send, list_recv, row_send, row_recv, own_sem
+):
+    me = lax.axis_index("dev")
+    place, core = coords_of(me)
+    count, cap = picked.shape[:2]
+    barrier = pltpu.get_barrier_semaphore()
+
+    def greet(step, carry):
+        other = peer_of(place, core, step)
+        pl.semaphore_signal(barrier, inc=1, device_id=(other,), device_id_type=MESH)
+        return carry
+
+    lax.fori_loop(1, count, greet, 0)
+    pl.semaphore_wait(barrier, count - 1)
+
+    def list_copy(other):
+        return pltpu.make_async_remote_copy(
+            src_ref=lists.at[other],
+            dst_ref=got.at[me],
+            send_sem=list_send,
+            recv_sem=list_recv,
+            device_id=(other,),
+            device_id_type=MESH,
+        )
+
+    def row_copy(other):
+        return pltpu.make_async_remote_copy(
+            src_ref=picked.at[other],
+            dst_ref=arrived.at[me],
+            send_sem=row_send,
+            recv_sem=row_recv,
+            device_id=(other,),
+            device_id_type=MESH,
+        )
+
+    def all_of(source, target, send_sem, recv_sem):
+        return pltpu.make_async_remote_copy(
+            src_ref=source.at[pl.ds(0, count - 1)],
+            dst_ref=target.at[pl.ds(0, count - 1)],
+            send_sem=send_sem,
+            recv_sem=recv_sem,
+            device_id=(device_of(place, 1 - core),),
+            device_id_type=MESH,
+        )
+
+    def send_list(step, carry):
+        list_copy(peer_of(place, core, step)).start()
+        return carry
+
+    lax.fori_loop(1, count, send_list, 0)
+    own = pltpu.make_async_copy(lists.at[me], got.at[me], own_sem)
+    own.start()
+    own.wait()
+    all_lists = all_of(lists, got, list_send, list_recv)
+    all_lists.wait_recv()
+    read = pltpu.make_async_copy(got, asked, own_sem)
+    read.start()
+    read.wait()
+
+    def pick(other):
+        for j in range(cap):
+            block[pl.ds(j, 1), :] = table[pl.ds(asked[other, 0, j], 1), :]
+        return block[...].astype(jnp.bfloat16)
+
+    def pick_send(step, carry):
+        other = peer_of(place, core, step)
+        picked[other] = pick(other)
+
+        @pl.when(step > 1)
+        def _():
+            row_copy(peer_of(place, core, step - 1)).start()
+
+        return carry
+
+    lax.fori_loop(1, count, pick_send, 0)
+    arrived[me] = pick(me)
+    row_copy(peer_of(place, core, count - 1)).start()
+    all_rows = all_of(picked, arrived, row_send, row_recv)
+    all_rows.wait_recv()
+    all_rows.wait_send()
+    all_lists.wait_send()
+
+
+def fetch_all(lists, table):
+    count, cap = lists.shape
+    emb = table.shape[1]
+    vmem = pl.BlockSpec(memory_space=pltpu.VMEM)
+    padded = jnp.pad(lists, ((0, 0), (0, emb - cap))).reshape(count, 1, emb)
+    fetched, got = pl.pallas_call(
+        fetch_kernel,
+        out_shape=(
+            jax.ShapeDtypeStruct((count, cap, emb), jnp.bfloat16),
+            jax.ShapeDtypeStruct((count, 1, emb), jnp.int32),
+        ),
+        in_specs=[vmem] * 2,
+        out_specs=(vmem, vmem),
+        scratch_shapes=[
+            pltpu.SMEM((count, 1, emb), jnp.int32),
+            pltpu.VMEM((count, cap, emb), jnp.bfloat16),
+            pltpu.VMEM((cap, emb), jnp.float32),
+        ]
+        + [pltpu.SemaphoreType.DMA(())] * 5,
+        compiler_params=pltpu.CompilerParams(
+            collective_id=1, has_side_effects=True, vmem_limit_bytes=24 * 2**20
+        ),
+        name="fetch_all",
+    )(padded, table)
+    return fetched, got[:, 0, :cap]
+
+
+def cross_kernel(
+    rows, ids, cot, hot, fetched, down, up, bias, part, cold, table, block, x_all, mix_all, grad, pair, slots
+):
+    samples, width = cot.shape
+    hot_rows, emb = hot.shape
+    owners, cap = fetched.shape[:2]
+    fields = width // emb
+    dense_cols = 2 * down.shape[1]
+    f32, bf16 = jnp.float32, jnp.bfloat16
+
+    def widen_hot(i, carry):
+        at = pl.ds(pl.multiple_of(i * 256, 256), 256)
+        table[at, :] = hot[at, :].astype(f32)
+        return carry
+
+    def widen_cold(i, carry):
+        at = pl.ds(pl.multiple_of(hot_rows + i * cap, 8), cap)
+        table[at, :] = fetched[i].astype(f32)
+        return carry
+
+    lax.fori_loop(0, hot_rows // 256, widen_hot, 0)
+    lax.fori_loop(0, owners, widen_cold, 0)
+
+    def gather_field(f, carry):
+        cols = pl.ds(pl.multiple_of(f * emb, emb), emb)
+
+        def gather_rows(i, inner):
+            base = pl.multiple_of(i * 16, 16)
+            for j in range(16):
+                block[pl.ds(base + j, 1), :] = table[pl.ds(rows[f, base + j], 1), :]
+            return inner
+
+        lax.fori_loop(0, samples // 16, gather_rows, 0)
+        x = block[...]
+        x_all[:, cols] = x.astype(bf16)
+        mix_all[:, cols] = (cot[:, cols].astype(f32) * x).astype(bf16)
+        return carry
+
+    lax.fori_loop(0, fields, gather_field, 0)
+    nt = (((1,), (1,)), ((), ()))
+    tn = (((0,), (0,)), ((), ()))
+    latent = jnp.dot(x_all[...], down[...], preferred_element_type=f32).astype(bf16)
+    back = lax.dot_general(mix_all[...], up[...], nt, preferred_element_type=f32).astype(bf16)
+    ones = jnp.ones((samples, emb), bf16)
+    latent_one = jnp.concatenate([latent, ones], axis=1)
+
+    def per_chunk(n, carry):
+        cols = pl.ds(pl.multiple_of(n * 256, 256), 256)
+        mixing = jnp.dot(latent, up[:, cols], preferred_element_type=f32) + bias[:, cols]
+        from_back = lax.dot_general(back, down[cols, :], nt, preferred_element_type=f32)
+        g = cot[:, cols].astype(f32) * (mixing + 1.0) + from_back
+        for h in range(2):
+            at = pl.ds(pl.multiple_of((2 * n + h) * samples, samples), samples)
+            piece = g[:, h * emb : (h + 1) * emb]
+            grad[at, :] = piece
+            high = piece.astype(bf16)
+            pair[at, :emb] = high
+            pair[at, emb:] = (piece - high.astype(f32)).astype(bf16)
+        part[cols, : dense_cols // 2] = lax.dot_general(
+            x_all[:, cols], back, tn, preferred_element_type=f32
+        ).astype(bf16)
+        up_part = lax.dot_general(
+            mix_all[:, cols], latent_one, tn, preferred_element_type=f32
+        ).astype(bf16)
+        part[cols, dense_cols // 2 : dense_cols] = up_part[:, : dense_cols // 2]
+        part[cols, dense_cols + emb :] = up_part[:, dense_cols // 2 :]
+        return carry
+
+    lax.fori_loop(0, width // 256, per_chunk, 0)
+    slots[...] = jnp.zeros_like(slots)
+
+    def place_field(f, carry):
+        def place_rows(i, inner):
+            base = pl.multiple_of(i * 16, 16)
+            for j in range(16):
+                row = rows[f, base + j]
+                to = jnp.where(row >= hot_rows, row - hot_rows, owners * cap)
+                slots[pl.ds(to, 1), :] = grad[pl.ds(f * samples + base + j, 1), :]
+            return inner
+
+        lax.fori_loop(0, samples // 16, place_rows, 0)
+        return carry
+
+    lax.fori_loop(0, fields, place_field, 0)
+
+    def narrow(i, carry):
+        cold[i] = slots[pl.ds(pl.multiple_of(i * cap, 8), cap), :].astype(bf16)
+        return carry
+
+    lax.fori_loop(0, owners, narrow, 0)
+
+    def hot_tile(t, carry):
+        first = pl.multiple_of(t * 256, 256)
+        mine = first + lax.broadcasted_iota(jnp.int32, (256, samples), 0)
+        acc = jnp.zeros((256, 2 * emb), f32)
+        for f in range(fields):
+            mask = jnp.where(mine == ids[f : f + 1, :], 1.0, 0.0).astype(bf16)
+            acc = acc + jnp.dot(
+                mask, pair[f * samples : (f + 1) * samples, :], preferred_element_type=f32
+            )
+        part[pl.ds(first, 256), dense_cols : dense_cols + emb] = (
+            acc[:, :emb] + acc[:, emb:]
+        ).astype(bf16)
+        return carry
+
+    lax.fori_loop(0, hot_rows // 256, hot_tile, 0)
+
+
+def cross_layer(rows, ids, cot, hot, fetched, down, up, bias):
+    samples, width = cot.shape
+    hot_rows, emb = hot.shape
+    owners, cap = fetched.shape[:2]
+    vmem = pl.BlockSpec(memory_space=pltpu.VMEM)
+    return pl.pallas_call(
+        cross_kernel,
+        out_shape=(
+            jax.ShapeDtypeStruct((width, 2 * down.shape[1] + 2 * emb), jnp.bfloat16),
+            jax.ShapeDtypeStruct((owners, cap, emb), jnp.bfloat16),
+        ),
+        in_specs=[pl.BlockSpec(memory_space=pltpu.SMEM)] + [vmem] * 7,
+        out_specs=(vmem, vmem),
+        scratch_shapes=[
+            pltpu.VMEM((hot_rows + owners * cap, emb), jnp.float32),
+            pltpu.VMEM((samples, emb), jnp.float32),
+            pltpu.VMEM((samples, width), jnp.bfloat16),
+            pltpu.VMEM((samples, width), jnp.bfloat16),
+            pltpu.VMEM((samples * width // emb, emb), jnp.float32),
+            pltpu.VMEM((samples * width // emb, 2 * emb), jnp.bfloat16),
+            pltpu.VMEM((owners * cap + 8, emb), jnp.float32),
+        ],
+        compiler_params=pltpu.CompilerParams(vmem_limit_bytes=56 * 2**20),
+        name="cross_layer",
+    )(rows, ids, cot, hot, fetched, down, up, bias)
+
 
 def body(
     cotangent,
@@ -202,48 +453,29 @@
     fetch_rows,
 ):
     devices = lax.axis_size("dev")
-    sample_count, fields = hot_ids.shape
     slab_rows, emb_width = cold_table.shape
     hot_rows = hot_table.shape[0]
     capacity = fetch_rows.shape[2]
     cross_width = cross_down.shape[0]
     shard_rows = dense_master.shape[0]
     scale_mean = 1.0 / devices
-    requests = lax.all_to_all(fetch_rows, "dev", split_axis=1, concat_axis=0, tiled=True)
-    request_flat = requests.reshape(devices * capacity)
-    picked = jnp.take(cold_table, request_flat, axis=0).astype(jnp.bfloat16)
-    fetched = lax.all_to_all(
-        picked.reshape(devices, capacity, emb_width), "dev", split_axis=0, concat_axis=0, tiled=True
-    )
-    fetched_flat = fetched.reshape(devices * capacity, emb_width)
+    fetched, asked = fetch_all(fetch_rows[0], cold_table)
+    request_flat = asked.reshape(devices * capacity)
     is_hot = lookup_slot < 0
-    cold_pos = jnp.maximum(lookup_slot, 0)
-    chosen = jnp.where(
-        is_hot[..., None],
-        jnp.take(hot_table, hot_ids, axis=0),
-        jnp.take(fetched_flat, cold_pos, axis=0),
-    )
-    inputs = chosen.reshape(sample_count, cross_width)
-    latent = jnp.dot(inputs, cross_down, preferred_element_type=jnp.float32).astype(jnp.bfloat16)
-    mixing = jnp.dot(latent, cross_up, preferred_element_type=jnp.float32) + cross_bias
-    grad_f32 = cotangent.astype(jnp.float32)
-    grad_mix = (grad_f32 * inputs.astype(jnp.float32)).astype(jnp.bfloat16)
-    grad_latent = lax.dot_general(
-        grad_mix, cross_up, (((1,), (1,)), ((), ())), preferred_element_type=jnp.float32
-    ).astype(jnp.bfloat16)
-    back_part = lax.dot_general(
-        grad_latent, cross_down, (((1,), (1,)), ((), ())), preferred_element_type=jnp.float32
-    )
-    grad_input = grad_f32 * (mixing + 1.0) + back_part
-    per_lookup = grad_input.reshape(sample_count * fields, emb_width)
-    cold_target = jnp.where(is_hot, devices * capacity, lookup_slot).reshape(-1)
-    cold_part = (
-        jnp.zeros((devices * capacity, emb_width), jnp.float32)
-        .at[cold_target]
-        .add(per_lookup, mode="drop")
+    lookup_rows = jnp.where(is_hot, hot_ids, hot_rows + lookup_slot).T
+    hot_only = jnp.where(is_hot, hot_ids, -1).T
+    part, cold_part = cross_layer(
+        lookup_rows,
+        hot_only,
+        cotangent,
+        hot_table,
+        fetched,
+        cross_down,
+        cross_up,
+        cross_bias.reshape(1, cross_width),
     )
     returned = lax.all_to_all(
-        cold_part.reshape(devices, capacity, emb_width).astype(jnp.bfloat16),
+        cold_part,
         "dev",
         split_axis=0,
         concat_axis=0,
@@ -257,19 +489,6 @@
     cold_new, cold_m_new, cold_v_new = adam_update(
         cold_table, cold_m, cold_v, cold_sum * scale_mean
     )
-    hot_target = jnp.where(is_hot, hot_ids, hot_rows).reshape(-1)
-    hot_part = (
-        jnp.zeros((hot_rows, emb_width), jnp.float32).at[hot_target].add(per_lookup, mode="drop")
-    )
-    bias_part = jnp.sum(grad_mix.astype(jnp.float32), axis=0)
-    down_part = lax.dot_general(
-        inputs, grad_latent, (((0,), (0,)), ((), ())), preferred_element_type=jnp.float32
-    )
-    up_part = lax.dot_general(
-        grad_mix, latent, (((0,), (0,)), ((), ())), preferred_element_type=jnp.float32
-    )
-    column = jnp.pad(bias_part[:, None], ((0, 0), (0, emb_width - 1)))
-    part = jnp.concatenate([down_part, up_part, hot_part, column], axis=1).astype(jnp.bfloat16)
     gathered, master_new, dense_m_new, dense_v_new = reduce_all(
         part.reshape(4, 4, 4, 2, shard_rows, part.shape[1]), dense_master, dense_m, dense_v
     )

time: 264 us -> 187 us (0.71)
  Pallas kernels: 62.6 us -> 145 us
  other arithmetic: 89.5 us -> 25.1 us
  local copies, waits for them, and re-layouts: 56.7 us -> 8.7 us
  starting transfers between devices: 26.9 us -> 6.54 us
  waiting for transfers between devices: 16.2 us -> 0.01 us
  matrix products: 10.6 us -> 0 us
    pallas_call x0 -> x2, Pallas kernels: none -> 82.6 us  [the longest x1 44.5 us: cross_layer(): pl.pallas_call(cross_kernel, out_shape=(jax.ShapeDtypeStruct((width, 2 *...]
    scatter-add x2 -> x0, other arithmetic: 46.9 us -> none  [the longest x1 23.9 us: body(): cold_part = jnp.zeros((devices * capacity, emb_width), jnp.float32).at[co...]
    gather x3 -> x0, local copies, waits for them, and re-layouts: 39.6 us -> none  [the longest x1 15 us: body(): jnp.take(hot_table, hot_ids, axis=0)]
    all_to_all x3 -> x1, starting transfers between devices: 26.9 us -> 6.54 us  [body(): lax.all_to_all(cold_part, 'dev', split_axis=0, concat_axis=0, tiled=True)]
    all_to_all x3 -> x1, waiting for transfers between devices: 16.2 us -> 0.01 us  [body(): lax.all_to_all(cold_part, 'dev', split_axis=0, concat_axis=0, tiled=True)]
    dot_general x6 -> x0, matrix products: 10.6 us -> none  [the longest x1 3.55 us: body(): lax.dot_general(grad_mix, latent, (((0,), (0,)), ((), ())), preferred_ele...]
    select_n x6 -> x1, other arithmetic: 6.95 us -> 0.01 us  [body(): cold_sum = jnp.zeros((slab_rows, emb_width), jnp.float32).at[request_flat...]
    concatenate x1 -> x0, other arithmetic: 4.22 us -> none  [body(): jnp.concatenate([down_part, up_part, hot_part, column], axis=1)]
  transfers between devices with their start and end apart: 3 -> 1, of which waited for: 1 -> 0; matrix products, arithmetic and copies ran while one was open for 11% -> 3% of each run, Pallas kernels for 24% -> 34%
where the time goes in v2:
time: 187 us; the launch traced here: 186 us
  Pallas kernels  145 us (78%)
  other arithmetic  25.1 us (13%)
  local copies, waits for them, and re-layouts  8.7 us (5%)
  starting transfers between devices  6.54 us (3%)
    pallas_call x1, Pallas kernels, reduce_all(): pl.pallas_call(reduce_kernel, out_shape=(jax.ShapeDtypeStruct(part.shape,...  62.4 us
    pallas_call x1, Pallas kernels, cross_layer(): pl.pallas_call(cross_kernel, out_shape=(jax.ShapeDtypeStruct((width, 2 *...  44.5 us
    pallas_call x1, Pallas kernels, fetch_all(): pl.pallas_call(fetch_kernel, out_shape=(jax.ShapeDtypeStruct((count, cap,...  38.1 us
    scatter-add x1, other arithmetic, body(): cold_sum = jnp.zeros((slab_rows, emb_width), jnp.float32).at[request_flat...  17.2 us
    all_to_all x1, starting transfers between devices, body(): lax.all_to_all(cold_part, 'dev', split_axis=0, concat_axis=0, tiled=True)  6.54 us
    unnamed x18, local copies, waits for them, and re-layouts  5.46 us
  transfers between devices with their start and end apart: 1, of which 0 were waited for; matrix products, arithmetic and copies ran while one was open for 3% of the time, Pallas kernels for 34%

profile of v2, /device:TPU:1, one launch (start us, length us, event | category | flops | bytes accessed | tf_op | source)
XLA Modules:
  0.0 186.1 jit_solution(8884935484739918939)
XLA Ops:
  0.6 0.8 copy.24
  1.5 0.0 copy-start.1
  1.5 1.2 copy-done.1
  2.7 38.1 %fetch_all.1 = (bf16[128,24,128]{2,1,0:T(8,128)(2,1)S(1)}, s32[128,1,128]{2,1,0:T(1,128)S(1)}) custom-call(s32[128,1,128]{2,1,0:T(1,128)S(1)} %bitcast.15, f32[2048,128]{1,0:T(8,128)S(1)} %copy-done.1), custom_call_target="tpu_custom_call" | custom-call | tf_op jit(solution)/shard_map/fetch_all/pallas_call | solution.py:282
  40.8 0.0 copy-start.3
  40.8 0.9 copy-done.3
  41.7 1.3 select_bitcast_fusion
  43.0 0.0 copy-start.4
  43.0 0.0 copy-start.5
  43.0 0.0 copy-start.6
  43.0 44.5 %cross_layer.1 = (bf16[2048,1280]{1,0:T(8,128)(2,1)}, bf16[128,24,128]{2,1,0:T(8,128)(2,1)}) custom-call(s32[16,256]{1,0:T(8,128)} %get-tuple-element.29.rows, s32[16,256]{1,0:T(8,128)} %get-tuple-element.28.ids, bf16[256,2048]{1,0:T(8,128)(2,1)} %cot.1, bf16[2048,128]{1,0:T(8,128)(2,1)} %hot.1, bf16[128,24,128]{2,1,0:T(8,128)(2,1)} %copy-done.3, ...), custom_call_target="tpu_custom_call" | custom-call | tf_op jit(solution)/shard_map/cross_layer/pallas_call | solution.py:417
  87.5 6.5 %all-to-all-start = ((bf16[128,24,128]{2,1,0:T(8,128)(2,1)}), bf16[128,24,128]{2,1,0:T(8,128)(2,1)S(1)}, u32[]{:S(2)}, u32[]{:S(2)}) async-start(bf16[128,24,128]{2,1,0:T(8,128)(2,1)} %get-tuple-element.21), calls=%async_computation | async-start | bytes 1572864 | tf_op jit(solution)/shard_map/all_to_all | solution.py:477
  94.1 0.0 copy-done.4
  94.1 0.0 copy-done.5
  94.1 0.0 copy-done.6
  94.1 62.4 %reduce_all.1 = (bf16[4,4,4,2,16,1280]{5,4,3,2,1,0:T(8,128)(2,1)S(1)}, f32[16,1024]{1,0:T(8,128)S(1)}, f32[16,1024]{1,0:T(8,128)S(1)}, f32[16,1024]{1,0:T(8,128)S(1)}) custom-call(bf16[4,4,4,2,16,1280]{5,4,3,2,1,0:T(8,128)(2,1)} %bitcast.16, f32[16,1024]{1,0:T(8,128)S(1)} %copy-done.4, f32[16,1024]{1,0:T(8,128)S(1)} %copy-done.5, f32[16,1024]{1,0:T(8,128)S(1)} %copy-done.6), custom_call_target="tpu_custom_call" | custom-call | tf_op jit(solution)/shard_map/reduce_all/pallas_call | solution.py:168
  156.5 0.0 copy-start
  156.5 3.0 %slice.18 = bf16[2048,1024]{1,0:T(8,128)(2,1)} slice(bf16[2048,1280]{1,0:T(8,128)(2,1)S(1)} %bitcast.12), slice={[0:2048], [0:1024]} | slice | bytes 8388608 | tf_op jit(solution)/shard_map/slice | solution.py:499
  159.5 0.7 copy-done
  160.1 0.0 copy-start.2
  160.1 1.0 slice_convert_fusion
  161.2 0.2 slice_reduce_fusion
  161.4 0.1 reshape_squeeze.3
  161.5 1.9 convert_reduce_fusion
  163.3 0.0 all-to-all-done
  163.3 17.2 %scatter_custom_fusion = f32[2048,128]{1,0:T(8,128)S(1)} fusion(s32[3072]{0:T(1024)S(1)} %bitcast.19, bf16[3072,128]{1,0:T(8,128)(2,1)S(1)} %bitcast.17, f32[]{:T(128)} %constant.5.clone.1), kind=kCustom, calls=%fused_computation.1 | custom fusion | flops 786432 | bytes 1835012 | tf_op jit(solution)/shard_map/scatter-add | solution.py:487
  180.6 0.0 copy-done.2
  180.6 3.6 %divide_subtract_fusion = (f32[2048,128]{1,0:T(8,128)}, f32[2048,128]{1,0:T(8,128)}, f32[2048,128]{1,0:T(8,128)}) fusion(f32[2048,128]{1,0:T(8,128)S(1)} %copy-done.2, f32[2048,128]{1,0:T(8,128)S(1)} %scatter_custom_fusion, f32[2048,128]{1,0:T(8,128)} %param.17, f32[2048,128]{1,0:T(8,128)} %param.18), kind=kLoop, calls=%fused_computation.4 | loop fusion | flops 3407872 | bytes 7340032 | tf_op jit(solution)/shard_map/sub | solution.py:21
  184.2 0.6 copy.28
  184.8 0.6 copy.29
  185.4 0.6 copy.30
  (2 shorter events, 0.0 us)
Async XLA Ops:
  1.5 1.2 copy-start.1
  40.8 0.9 copy-start.3
  43.0 51.0 %copy-start.4 = (f32[16,1024]{1,0:T(8,128)S(1)}, f32[16,1024]{1,0:T(8,128)}, u32[]{:S(2)}) copy-start(f32[16,1024]{1,0:T(8,128)} %master.1) | copy-start | bytes 196612
  43.0 51.0 %copy-start.5 = (f32[16,1024]{1,0:T(8,128)S(1)}, f32[16,1024]{1,0:T(8,128)}, u32[]{:S(2)}) copy-start(f32[16,1024]{1,0:T(8,128)} %m_in.1) | copy-start | bytes 196612
  43.0 51.1 %copy-start.6 = (f32[16,1024]{1,0:T(8,128)S(1)}, f32[16,1024]{1,0:T(8,128)}, u32[]{:S(2)}) copy-start(f32[16,1024]{1,0:T(8,128)} %v_in.1) | copy-start | bytes 196612
  87.5 75.8 %all-to-all-start = ((bf16[128,24,128]{2,1,0:T(8,128)(2,1)}), bf16[128,24,128]{2,1,0:T(8,128)(2,1)S(1)}, u32[]{:S(2)}, u32[]{:S(2)}) async-start(bf16[128,24,128]{2,1,0:T(8,128)(2,1)} %get-tuple-element.21), calls=%async_computation | async-start | bytes 1572864 | tf_op jit(solution)/shard_map/all_to_all | solution.py:477
  156.5 3.6 %copy-start = (bf16[4,4,4,2,16,1280]{5,4,3,2,1,0:T(8,128)(2,1)}, bf16[4,4,4,2,16,1280]{5,4,3,2,1,0:T(8,128)(2,1)S(1)}, u32[]{:S(2)}) copy-start(bf16[4,4,4,2,16,1280]{5,4,3,2,1,0:T(8,128)(2,1)S(1)} %get-tuple-element.19) | copy-start | bytes 15728644
  160.1 20.4 %copy-start.2 = (f32[2048,128]{1,0:T(8,128)S(1)}, f32[2048,128]{1,0:T(8,128)}, u32[]{:S(2)}) copy-start(f32[2048,128]{1,0:T(8,128)} %table.1) | copy-start | bytes 3145732

commit v3 on v1

v3 whole, which is shorter than its diff:
```python
import jax
import jax.numpy as jnp
from jax import lax
from jax.experimental import pallas as pl
from jax.experimental.pallas import tpu as pltpu
from jax.sharding import PartitionSpec as P

MESH = pl.DeviceIdType.MESH

first_decay = 0.9
second_decay = 0.999
adam_epsilon = 1e-08
learn_rate = 0.01
first_fix = 1.0 - (0.9**10) ** 10
second_fix = 1.0 - (0.999**10) ** 10


def adam_update(params, moment_one, moment_two, gradient):
    moment_one = first_decay * moment_one + (1.0 - first_decay) * gradient
    moment_two = second_decay * moment_two + (1.0 - second_decay) * gradient * gradient
    params = params - learn_rate * (moment_one / first_fix) / (
        jnp.sqrt(moment_two / second_fix) + adam_epsilon
    )
    return (params, moment_one, moment_two)

CUTS = ((0, 384), (384, 768), (768, 1152))
ORDERS = ((0, 1, 2), (1, 2, 0), (2, 0, 1))


def coords_of(me):
    return [me // 32, lax.rem(me // 8, 4), lax.rem(me // 2, 4)], lax.rem(me, 2)


def device_of(place, core):
    return place[0] * 32 + place[1] * 8 + place[2] * 2 + core


def moved(place, axis, step):
    return [lax.rem(p + step, 4) if a == axis else p for a, p in enumerate(place)]


def visit_peers(place, core, visit):
    tails = [lax.rem(place[2] + s, 4) * 2 + c for s in range(4) for c in (core, 1 - core)]

    def along_z(i, carry):
        z = lax.rem(place[0] + i, 4) * 32

        def along_x(j, inner):
            base = z + lax.rem(place[1] + j, 4) * 8
            visit([base + tail for tail in tails], i + j > 0)
            return inner

        return lax.fori_loop(0, 4, along_x, carry)

    lax.fori_loop(0, 4, along_z, 0)


def for_peers(place, core, act):
    def visit(others, away):
        pl.when(away)(lambda: act(others[0]))
        for other in others[1:]:
            act(other)

    visit_peers(place, core, visit)


def meet_all(place, core):
    barrier = pltpu.get_barrier_semaphore()
    for_peers(
        place,
        core,
        lambda other: pl.semaphore_signal(
            barrier, inc=1, device_id=(other,), device_id_type=MESH
        ),
    )
    pl.semaphore_wait(barrier, 127)


def remote(source, target, send_sem, recv_sem, other):
    return pltpu.make_async_remote_copy(
        src_ref=source,
        dst_ref=target,
        send_sem=send_sem,
        recv_sem=recv_sem,
        device_id=(other,),
        device_id_type=MESH,
    )


def fetch_kernel(
    lists, table, arrived, got, asked, picked, block, list_send, list_recv, row_send, row_recv, own_sem
):
    me = lax.axis_index("dev")
    place, core = coords_of(me)
    partner = device_of(place, 1 - core)
    count, cap = picked.shape[:2]
    most = pl.ds(0, count - 1)
    meet_all(place, core)
    for_peers(
        place,
        core,
        lambda other: remote(lists.at[other], got.at[me], list_send, list_recv, other).start(),
    )
    own = pltpu.make_async_copy(lists.at[me], got.at[me], own_sem)
    own.start()
    own.wait()
    all_lists = remote(lists.at[most], got.at[most], list_send, list_recv, partner)
    all_lists.wait_recv()
    read = pltpu.make_async_copy(got, asked, own_sem)
    read.start()
    read.wait()

    def pick(other, k):
        for j in range(cap):
            block[k, pl.ds(j, 1), :] = table[pl.ds(asked[other, 0, j], 1), :]
        picked[other] = block[k].astype(jnp.bfloat16)

    def send(other):
        remote(picked.at[other], arrived.at[me], row_send, row_recv, other).start()

    def visit(others, away):
        for k, other in enumerate(others):
            pick(other, k)
        pl.when(away)(lambda: send(others[0]))
        for other in others[1:]:
            send(other)

    visit_peers(place, core, visit)
    arrived[me] = picked[me]
    all_rows = remote(picked.at[most], arrived.at[most], row_send, row_recv, partner)
    all_rows.wait_recv()
    all_rows.wait_send()
    all_lists.wait_send()


def fetch_all(lists, table):
    count, cap = lists.shape
    emb = table.shape[1]
    vmem = pl.BlockSpec(memory_space=pltpu.VMEM)
    padded = jnp.pad(lists, ((0, 0), (0, emb - cap))).reshape(count, 1, emb)
    fetched, got = pl.pallas_call(
        fetch_kernel,
        out_shape=(
            jax.ShapeDtypeStruct((count, cap, emb), jnp.bfloat16),
            jax.ShapeDtypeStruct((count, 1, emb), jnp.int32),
        ),
        in_specs=[vmem] * 2,
        out_specs=(vmem, vmem),
        scratch_shapes=[
            pltpu.SMEM((count, 1, emb), jnp.int32),
            pltpu.VMEM((count, cap, emb), jnp.bfloat16),
            pltpu.VMEM((8, cap, emb), jnp.float32),
        ]
        + [pltpu.SemaphoreType.DMA(())] * 5,
        compiler_params=pltpu.CompilerParams(
            collective_id=1, has_side_effects=True, vmem_limit_bytes=24 * 2**20
        ),
        name="fetch_all",
    )(padded, table)
    return fetched, got[:, 0, :cap]


def reduce_kernel(
    part,
    bias,
    master,
    m_in,
    v_in,
    cold,
    slots,
    cold_table,
    cold_m,
    cold_v,
    out,
    bias_out,
    master_out,
    m_out,
    v_out,
    cold_out,
    cold_m_out,
    cold_v_out,
    *rest,
):
    first, sums0, got1, sums1, got2, sums2, got3 = (rest[3 * i : 3 * i + 3] for i in range(7))
    total, bias_sum, bias_got, returned, wide, flat = rest[21:27]
    send_sem, recv_sem, cold_send, cold_recv, own_sem = rest[27:]
    me = lax.axis_index("dev")
    place, core = coords_of(me)
    partner = device_of(place, 1 - core)
    count, cap, emb = cold.shape
    dense = master.shape[1]
    scale = 1.0 / count
    f32, bf16 = jnp.float32, jnp.bfloat16
    meet_all(place, core)
    started = []

    def send(src, dst, color, phase, slot, other):
        copy = remote(
            src, dst, send_sem.at[color, phase, slot], recv_sem.at[color, phase, slot], other
        )
        copy.start()
        started.append(copy)
        return copy

    def slab(axis, at, free):
        return tuple(at if a == axis else slice(None) for a in free)

    waiting = {}
    for k, (low, high) in enumerate(CUTS):
        waiting[k] = [
            send(part.at[:, :, :, 1 - core, :, low:high], first[k], k, 0, 0, partner)
        ]
    waiting[3] = [send(bias, bias_got.at[0, 0], 3, 0, 0, partner)]
    for_peers(
        place,
        core,
        lambda other: remote(cold.at[other], returned.at[me], cold_send, cold_recv, other).start(),
    )
    own = pltpu.make_async_copy(cold.at[me], returned.at[me], own_sem)
    own.start()
    own.wait()
    for phase in range(4):
        for k, (low, high) in enumerate(CUTS):
            axis = ORDERS[k][phase] if phase < 3 else None
            free = [a for a in range(3) if a not in ORDERS[k][: phase - 1]] if phase else None
            for copy in waiting[k]:
                copy.wait_recv()
            if phase == 0:

                def add_first(i, carry):
                    for x in range(4):
                        mine = part[i, x, :, core, :, low:high].astype(f32)
                        sums0[k][i, x] = (mine + first[k][i, x].astype(f32)).astype(bf16)
                    return carry

                lax.fori_loop(0, 4, add_first, 0)
            else:
                before = ORDERS[k][phase - 1]
                source = (sums0, sums1, sums2)[phase - 1][k]
                got = (got1, got2, got3)[phase - 1][k]
                mine = source[slab(before, place[before], free)].astype(f32)
                for slot in range(3):
                    mine = mine + got[slot].astype(f32)
                if phase < 3:
                    (sums1, sums2)[phase - 1][k][...] = mine.astype(bf16)
                else:
                    total[:, low:high] = mine
            if phase < 3:
                source = (sums0, sums1, sums2)[phase][k]
                into = (got1, got2, got3)[phase][k]
                left = [a for a in range(3) if a not in ORDERS[k][:phase]]
                waiting[k] = [
                    send(
                        source.at[slab(axis, moved(place, axis, s)[axis], left)],
                        into.at[s - 1],
                        k,
                        1 + phase,
                        s - 1,
                        device_of(moved(place, axis, s), core),
                    )
                    for s in (1, 2, 3)
                ]
        for copy in waiting[3]:
            copy.wait_recv()
        if phase == 0:
            bias_sum[0] = bias[...] + bias_got[0, 0]
        else:
            bias_sum[phase] = (bias_sum[phase - 1] + bias_got[phase, 0]) + (
                bias_got[phase, 1] + bias_got[phase, 2]
            )
        if phase < 3:
            waiting[3] = [
                send(
                    bias_sum.at[phase],
                    bias_got.at[phase + 1, s - 1],
                    3,
                    1 + phase,
                    s - 1,
                    device_of(moved(place, phase, s), core),
                )
                for s in (1, 2, 3)
            ]
    bias_out[...] = bias_sum[3] * scale
    new, m_new, v_new = adam_update(master[...], m_in[...], v_in[...], total[:, :dense] * scale)
    master_out[...] = new
    m_out[...] = m_new
    v_out[...] = v_new
    out[place[0], place[1], place[2], core, :, :dense] = new.astype(bf16)
    out[place[0], place[1], place[2], core, :, dense:] = (total[:, dense:] * scale).astype(bf16)

    def update_cold():
        most = pl.ds(0, count - 1)
        all_cold = remote(cold.at[most], returned.at[most], cold_send, cold_recv, partner)
        all_cold.wait_recv()

        def widen(i, carry):
            wide[pl.ds(pl.multiple_of(i * cap, 8), cap), :] = returned[i].astype(f32)
            return carry

        lax.fori_loop(0, count, widen, 0)
        flat[...] = wide[...].astype(bf16)

        def update_tile(t, carry):
            at = pl.ds(pl.multiple_of(t * 256, 256), 256)
            mine = t * 256 + lax.broadcasted_iota(jnp.int32, (256, 512), 0)
            acc = jnp.zeros((256, emb), f32)
            for c in range(count * cap // 512):
                mask = jnp.where(mine == slots[:, c * 512 : (c + 1) * 512], 1.0, 0.0).astype(bf16)
                acc = acc + jnp.dot(
                    mask, flat[c * 512 : (c + 1) * 512, :], preferred_element_type=f32
                )
            new, m_new, v_new = adam_update(
                cold_table[at, :], cold_m[at, :], cold_v[at, :], acc * scale
            )
            cold_out[at, :] = new
            cold_m_out[at, :] = m_new
            cold_v_out[at, :] = v_new
            return carry

        lax.fori_loop(0, cold_table.shape[0] // 256, update_tile, 0)
        all_cold.wait_send()

    for phase in range(4):
        for k, (low, high) in enumerate(CUTS):
            order = ORDERS[k]
            for copy in waiting[k] if phase else []:
                copy.wait_recv()
            spread = order[3 - phase :]
            at = tuple(slice(None) if a in spread else place[a] for a in range(3))
            block = out.at[at + (core, slice(None), slice(low, high))]
            if phase < 3:
                axis = order[2 - phase]
                waiting[k] = [
                    send(
                        block, block, k, 4 + phase, s - 1, device_of(moved(place, axis, s), core)
                    )
                    for s in (1, 2, 3)
                ]
            else:
                waiting[k] = [send(block, block, k, 7, 0, partner)]
        if phase == 2:
            update_cold()
    for k in range(3):
        for copy in waiting[k]:
            copy.wait_recv()
    for copy in started:
        copy.wait_send()


def reduce_all(part, bias, master, m_in, v_in, cold, slots, cold_table, cold_m, cold_v):
    widths = [high - low for low, high in CUTS]
    shapes = ((4, 4, 4), (4, 4, 4), (3, 4, 4), (4, 4), (3, 4), (4,), (3,))
    small = jax.ShapeDtypeStruct(master.shape, jnp.float32)
    slab = jax.ShapeDtypeStruct(cold_table.shape, jnp.float32)
    vmem = pl.BlockSpec(memory_space=pltpu.VMEM)
    count, cap, emb = cold.shape
    return pl.pallas_call(
        reduce_kernel,
        out_shape=(
            jax.ShapeDtypeStruct(part.shape, jnp.bfloat16),
            jax.ShapeDtypeStruct(bias.shape, jnp.float32),
        )
        + (small,) * 3
        + (slab,) * 3,
        in_specs=[vmem] * 10,
        out_specs=(vmem,) * 8,
        scratch_shapes=[
            pltpu.VMEM(shape + (16, width), jnp.bfloat16) for shape in shapes for width in widths
        ]
        + [
            pltpu.VMEM((16, part.shape[-1]), jnp.float32),
            pltpu.VMEM((4,) + bias.shape, jnp.float32),
            pltpu.VMEM((4, 3) + bias.shape, jnp.float32),
            pltpu.VMEM(cold.shape, jnp.bfloat16),
            pltpu.VMEM((count * cap, emb), jnp.float32),
            pltpu.VMEM((count * cap, emb), jnp.bfloat16),
            pltpu.SemaphoreType.DMA((4, 8, 3)),
            pltpu.SemaphoreType.DMA((4, 8, 3)),
        ]
        + [pltpu.SemaphoreType.DMA(())] * 3,
        compiler_params=pltpu.CompilerParams(
            collective_id=0, has_side_effects=True, vmem_limit_bytes=48 * 2**20
        ),
        name="reduce_all",
    )(part, bias, master, m_in, v_in, cold, slots, cold_table, cold_m, cold_v)


def cross_kernel(
    rows, puts, ids, cot, hot, fetched, down, up, bias, part, bias_part, cold, table, block, x_all, mix_all, grad, pair, slots
):
    samples, width = cot.shape
    hot_rows, emb = hot.shape
    owners, cap = fetched.shape[:2]
    fields = width // emb
    dense_cols = 2 * down.shape[1]
    f32, bf16 = jnp.float32, jnp.bfloat16

    def widen_hot(i, carry):
        at = pl.ds(pl.multiple_of(i * 256, 256), 256)
        table[at, :] = hot[at, :].astype(f32)
        return carry

    def widen_cold(i, carry):
        at = pl.ds(pl.multiple_of(hot_rows + i * cap, 8), cap)
        table[at, :] = fetched[i].astype(f32)
        return carry

    lax.fori_loop(0, hot_rows // 256, widen_hot, 0)
    lax.fori_loop(0, owners, widen_cold, 0)

    def gather_field(f, carry):
        cols = pl.ds(pl.multiple_of(f * emb, emb), emb)

        def gather_rows(i, inner):
            base = pl.multiple_of(i * 16, 16)
            first = f * samples + base
            for j in range(16):
                block[pl.ds(base + j, 1), :] = table[pl.ds(rows[first + j], 1), :]
            return inner

        lax.fori_loop(0, samples // 16, gather_rows, 0)
        x = block[...]
        x_all[:, cols] = x.astype(bf16)
        mix_all[:, cols] = (cot[:, cols].astype(f32) * x).astype(bf16)
        return carry

    lax.fori_loop(0, fields, gather_field, 0)
    nt = (((1,), (1,)), ((), ()))
    tn = (((0,), (0,)), ((), ()))
    latent = jnp.dot(x_all[...], down[...], preferred_element_type=f32).astype(bf16)
    back = lax.dot_general(mix_all[...], up[...], nt, preferred_element_type=f32).astype(bf16)
    ones = jnp.ones((8, samples), bf16)

    def per_chunk(n, carry):
        cols = pl.ds(pl.multiple_of(n * 256, 256), 256)
        mixing = jnp.dot(latent, up[:, cols], preferred_element_type=f32) + bias[:, cols]
        from_back = lax.dot_general(back, down[cols, :], nt, preferred_element_type=f32)
        g = cot[:, cols].astype(f32) * (mixing + 1.0) + from_back
        for h in range(2):
            at = pl.ds(pl.multiple_of((2 * n + h) * samples, samples), samples)
            piece = g[:, h * emb : (h + 1) * emb]
            grad[at, :] = piece
            high = piece.astype(bf16)
            pair[at, :emb] = high
            pair[at, emb:] = (piece - high.astype(f32)).astype(bf16)
        part[cols, : dense_cols // 2] = lax.dot_general(
            x_all[:, cols], back, tn, preferred_element_type=f32
        ).astype(bf16)
        part[cols, dense_cols // 2 : dense_cols] = lax.dot_general(
            mix_all[:, cols], latent, tn, preferred_element_type=f32
        ).astype(bf16)
        bias_part[:, cols] = jnp.dot(ones, mix_all[:, cols], preferred_element_type=f32)[:1]
        return carry

    lax.fori_loop(0, width // 256, per_chunk, 0)
    slots[...] = jnp.zeros_like(slots)

    def place_rows(i, carry):
        base = pl.multiple_of(i * 16, 16)
        for j in range(16):
            slots[pl.ds(puts[base + j], 1), :] = grad[pl.ds(base + j, 1), :]
        return carry

    lax.fori_loop(0, fields * samples // 16, place_rows, 0)

    def narrow(i, carry):
        cold[i] = slots[pl.ds(pl.multiple_of(i * cap, 8), cap), :].astype(bf16)
        return carry

    lax.fori_loop(0, owners, narrow, 0)

    def hot_tile(t, carry):
        first = pl.multiple_of(t * 256, 256)
        mine = first + lax.broadcasted_iota(jnp.int32, (256, samples), 0)
        acc = jnp.zeros((256, 2 * emb), f32)
        for f in range(fields):
            mask = jnp.where(mine == ids[f : f + 1, :], 1.0, 0.0).astype(bf16)
            acc = acc + jnp.dot(
                mask, pair[f * samples : (f + 1) * samples, :], preferred_element_type=f32
            )
        part[pl.ds(first, 256), dense_cols : dense_cols + emb] = (
            acc[:, :emb] + acc[:, emb:]
        ).astype(bf16)
        return carry

    lax.fori_loop(0, hot_rows // 256, hot_tile, 0)


def cross_layer(rows, puts, ids, cot, hot, fetched, down, up, bias):
    samples, width = cot.shape
    hot_rows, emb = hot.shape
    owners, cap = fetched.shape[:2]
    vmem = pl.BlockSpec(memory_space=pltpu.VMEM)
    return pl.pallas_call(
        cross_kernel,
        out_shape=(
            jax.ShapeDtypeStruct((width, 2 * down.shape[1] + emb), jnp.bfloat16),
            jax.ShapeDtypeStruct((1, width), jnp.float32),
            jax.ShapeDtypeStruct((owners, cap, emb), jnp.bfloat16),
        ),
        in_specs=[pl.BlockSpec(memory_space=pltpu.SMEM)] * 2 + [vmem] * 7,
        out_specs=(vmem,) * 3,
        scratch_shapes=[
            pltpu.VMEM((hot_rows + owners * cap, emb), jnp.float32),
            pltpu.VMEM((samples, emb), jnp.float32),
            pltpu.VMEM((samples, width), jnp.bfloat16),
            pltpu.VMEM((samples, width), jnp.bfloat16),
            pltpu.VMEM((samples * width // emb, emb), jnp.float32),
            pltpu.VMEM((samples * width // emb, 2 * emb), jnp.bfloat16),
            pltpu.VMEM((owners * cap + 8, emb), jnp.float32),
        ],
        compiler_params=pltpu.CompilerParams(vmem_limit_bytes=56 * 2**20),
        name="cross_layer",
    )(rows, puts, ids, cot, hot, fetched, down, up, bias)


def body(
    cotangent,
    hot_table,
    cold_table,
    cold_m,
    cold_v,
    cross_down,
    cross_up,
    cross_bias,
    dense_master,
    dense_m,
    dense_v,
    hot_ids,
    lookup_slot,
    fetch_rows,
):
    devices = lax.axis_size("dev")
    hot_rows = hot_table.shape[0]
    capacity = fetch_rows.shape[2]
    cross_width = cross_down.shape[0]
    shard_rows = dense_master.shape[0]
    fetched, asked = fetch_all(fetch_rows[0], cold_table)
    is_hot = lookup_slot < 0
    lookup_rows = jnp.where(is_hot, hot_ids, hot_rows + lookup_slot).T.reshape(-1)
    put_rows = jnp.where(is_hot, devices * capacity, lookup_slot).T.reshape(-1)
    hot_only = jnp.where(is_hot, hot_ids, -1).T
    part, bias_part, cold_part = cross_layer(
        lookup_rows,
        put_rows,
        hot_only,
        cotangent,
        hot_table,
        fetched,
        cross_down,
        cross_up,
        cross_bias.reshape(1, cross_width),
    )
    gathered, bias_grad, master_new, dense_m_new, dense_v_new, cold_new, cold_m_new, cold_v_new = reduce_all(
        part.reshape(4, 4, 4, 2, shard_rows, part.shape[1]),
        bias_part,
        dense_master,
        dense_m,
        dense_v,
        cold_part,
        asked.reshape(1, devices * capacity),
        cold_table,
        cold_m,
        cold_v,
    )
    flat = gathered.reshape(part.shape)
    dense_cols = dense_master.shape[1]
    hot_grad = flat[:, dense_cols:].astype(jnp.float32)
    bias_grad = bias_grad.reshape(cross_width)
    new_weights = flat[:, :dense_cols]
    return (
        hot_grad,
        bias_grad,
        cold_new,
        cold_m_new,
        cold_v_new,
        master_new,
        dense_m_new,
        dense_v_new,
        new_weights,
    )


def solution(mesh):
    return jax.shard_map(
        body,
        mesh=mesh,
        in_specs=(
            P("dev", None),
            P(),
            P("dev", None),
            P("dev", None),
            P("dev", None),
            P(),
            P(),
            P(),
            P("dev", None),
            P("dev", None),
            P("dev", None),
            P("dev", None),
            P("dev", None),
            P("dev", None, None),
        ),
        out_specs=(
            P(),
            P(),
            P("dev", None),
            P("dev", None),
            P("dev", None),
            P("dev", None),
            P("dev", None),
            P("dev", None),
            P(),
        ),
        check_vma=False,
    )
```

time: 264 us -> 144 us (0.55)
  other arithmetic: 89.5 us -> 3.47 us
  Pallas kernels: 62.6 us -> 123 us
  local copies, waits for them, and re-layouts: 56.7 us -> 16.3 us
  starting transfers between devices: 26.9 us -> 0 us
  waiting for transfers between devices: 16.2 us -> 0 us
  matrix products: 10.6 us -> 0 us
    scatter-add x3 -> x0, other arithmetic: 65.2 us -> none  [the longest x1 23.9 us: body(): cold_part = jnp.zeros((devices * capacity, emb_width), jnp.float32).at[co...]
    pallas_call x0 -> x2, Pallas kernels: none -> 58.8 us  [the longest x1 31.5 us: fetch_all(): pl.pallas_call(fetch_kernel, out_shape=(jax.ShapeDtypeStruct((count, cap,...]
    gather x3 -> x0, local copies, waits for them, and re-layouts: 39.6 us -> none  [the longest x1 15 us: body(): jnp.take(hot_table, hot_ids, axis=0)]
    all_to_all x3 -> x0, starting transfers between devices: 26.9 us -> none  [the longest x1 11.5 us: body(): lax.all_to_all(fetch_rows, 'dev', split_axis=1, concat_axis=0, tiled=True)]
    all_to_all x3 -> x0, waiting for transfers between devices: 16.2 us -> none  [the longest x1 16.2 us: body(): lax.all_to_all(picked.reshape(devices, capacity, emb_width), 'dev', split...]
    dot_general x6 -> x0, matrix products: 10.6 us -> none  [the longest x1 3.55 us: body(): lax.dot_general(grad_mix, latent, (((0,), (0,)), ((), ())), preferred_ele...]
    select_n x6 -> x0, other arithmetic: 6.95 us -> none  [the longest x1 5.45 us: body(): jnp.where(is_hot[..., None], jnp.take(hot_table, hot_ids, axis=0), jnp.ta...]
    unnamed x33 -> x26, local copies, waits for them, and re-layouts: 5.44 us -> 11.4 us
  transfers between devices with their start and end apart: 3 -> 0, of which waited for: 1 -> 0; matrix products, arithmetic and copies ran while one was open for 11% -> 0% of each run, Pallas kernels for 24% -> 0%
where the time goes in v3:
time: 144 us; the launch traced here: 143 us
  Pallas kernels  123 us (85%)
  local copies, waits for them, and re-layouts  16.3 us (11%)
  other arithmetic  3.47 us (2%)
    pallas_call x1, Pallas kernels, reduce_all(): pl.pallas_call(reduce_kernel, out_shape=(jax.ShapeDtypeStruct(part.shape,...  63.8 us
    pallas_call x1, Pallas kernels, fetch_all(): pl.pallas_call(fetch_kernel, out_shape=(jax.ShapeDtypeStruct((count, cap,...  31.5 us
    pallas_call x1, Pallas kernels, cross_layer(): pl.pallas_call(cross_kernel, out_shape=(jax.ShapeDtypeStruct((width, 2 *...  27.3 us
    unnamed x26, local copies, waits for them, and re-layouts  11.4 us
    slice x1, local copies, waits for them, and re-layouts, body(): new_weights = flat[:, :dense_cols]  4.64 us

profile of v3, /device:TPU:1, one launch (start us, length us, event | category | flops | bytes accessed | tf_op | source)
XLA Modules:
  0.0 143.1 jit_solution(10885294281243794808)
XLA Ops:
  0.6 0.0 copy-start.6
  0.7 0.0 copy-start.5
  0.7 0.0 copy-start.4
  0.7 1.4 select_bitcast_fusion
  2.1 0.6 copy.25
  2.7 0.6 copy.26
  3.3 0.8 copy.24
  4.1 0.0 copy-start
  4.1 1.2 copy-done
  5.3 0.0 copy-start.1
  5.3 31.5 %fetch_all.1 = (bf16[128,24,128]{2,1,0:T(8,128)(2,1)S(1)}, s32[128,1,128]{2,1,0:T(1,128)S(1)}) custom-call(s32[128,1,128]{2,1,0:T(1,128)S(1)} %bitcast.16, f32[2048,128]{1,0:T(8,128)S(1)} %copy-done), custom_call_target="tpu_custom_call" | custom-call | tf_op jit(solution)/shard_map/fetch_all/pallas_call | solution.py:141
  36.8 0.0 copy-start.2
  36.9 0.9 copy-done.2
  37.7 0.2 slice_reduce_fusion
  37.9 0.1 reshape_squeeze.3.slots
  38.0 27.3 %cross_layer.1 = (bf16[2048,1152]{1,0:T(8,128)(2,1)}, f32[1,2048]{1,0:T(1,128)}, bf16[128,24,128]{2,1,0:T(8,128)(2,1)}) custom-call(s32[4096]{0:T(1024)} %bitcast.22, s32[4096]{0:T(1024)} %bitcast.23, s32[16,256]{1,0:T(8,128)} %get-tuple-element.35.ids, bf16[256,2048]{1,0:T(8,128)(2,1)} %cot.1, bf16[2048,128]{1,0:T(8,128)(2,1)} %hot.1, ...), custom_call_target="tpu_custom_call" | custom-call | tf_op jit(solution)/shard_map/cross_layer/pallas_call | solution.py:494
  65.3 0.0 copy-done.6
  65.3 0.0 copy-done.5
  65.3 0.0 copy-done.4
  65.4 0.0 copy-done.1
  65.4 0.0 copy-start.3
  65.4 1.1 copy-done.3
  66.5 0.0 copy-start.7
  66.5 0.7 copy-done.7
  67.2 63.8 %reduce_all.1 = (bf16[4,4,4,2,16,1152]{5,4,3,2,1,0:T(8,128)(2,1)}, f32[1,2048]{1,0:T(1,128)S(1)}, f32[16,1024]{1,0:T(8,128)S(1)}, f32[16,1024]{1,0:T(8,128)S(1)}...) custom-call(bf16[4,4,4,2,16,1152]{5,4,3,2,1,0:T(8,128)(2,1)} %bitcast.20,, ...), custom_call_target="tpu_custom_call" | custom-call | tf_op jit(solution)/shard_map/reduce_all/pallas_call | solution.py:357
  131.0 2.1 %slice_convert_fusion = f32[2048,128]{1,0:T(8,128)} fusion(bf16[2048,1152]{1,0:T(8,128)(2,1)} %bitcast.18), kind=kLoop, calls=%fused_computation | loop fusion | flops 262144 | bytes 1572864 | tf_op jit(solution)/shard_map/convert_element_type | solution.py:568
  133.1 4.6 %slice.13 = bf16[2048,1024]{1,0:T(8,128)(2,1)} slice(bf16[2048,1152]{1,0:T(8,128)(2,1)} %bitcast.19), slice={[0:2048], [0:1024]} | slice | bytes 8388608 | tf_op jit(solution)/shard_map/slice | solution.py:570
  137.7 0.6 copy.34
  138.3 1.0 copy.35
  139.3 1.0 copy.36
  140.2 1.0 copy.37
  141.2 0.6 copy.38
  141.8 0.6 copy.39
  142.5 0.6 copy.40
  (1 shorter events, 0.0 us)
Async XLA Ops:
  0.6 64.7 %copy-start.6 = (f32[16,1024]{1,0:T(8,128)S(1)}, f32[16,1024]{1,0:T(8,128)}, u32[]{:S(2)}) copy-start(f32[16,1024]{1,0:T(8,128)} %v_in.1) | copy-start | bytes 196612
  0.7 64.7 %copy-start.5 = (f32[16,1024]{1,0:T(8,128)S(1)}, f32[16,1024]{1,0:T(8,128)}, u32[]{:S(2)}) copy-start(f32[16,1024]{1,0:T(8,128)} %m_in.1) | copy-start | bytes 196612
  0.7 64.7 %copy-start.4 = (f32[16,1024]{1,0:T(8,128)S(1)}, f32[16,1024]{1,0:T(8,128)}, u32[]{:S(2)}) copy-start(f32[16,1024]{1,0:T(8,128)} %master.1) | copy-start | bytes 196612
  4.1 1.2 copy-start
  5.3 60.0 %copy-start.1 = (f32[2048,128]{1,0:T(8,128)S(1)}, f32[2048,128]{1,0:T(8,128)}, u32[]{:S(2)}) copy-start(f32[2048,128]{1,0:T(8,128)} %cold_table.1) | copy-start | bytes 3145732
  36.8 0.9 copy-start.2
  65.4 1.1 copy-start.3
  66.5 0.7 copy-start.7

commit v4 on v0

v4 whole, which is shorter than its diff:
```python
import jax
import jax.numpy as jnp
from jax import lax
from jax.experimental import pallas as pl
from jax.experimental.pallas import tpu as pltpu
from jax.sharding import PartitionSpec as P

MESH = pl.DeviceIdType.MESH

first_decay = 0.9
second_decay = 0.999
adam_epsilon = 1e-08
learn_rate = 0.01
first_fix = 1.0 - (0.9**10) ** 10
second_fix = 1.0 - (0.999**10) ** 10


def adam_update(params, moment_one, moment_two, gradient):
    moment_one = first_decay * moment_one + (1.0 - first_decay) * gradient
    moment_two = second_decay * moment_two + (1.0 - second_decay) * gradient * gradient
    params = params - learn_rate * (moment_one / first_fix) / (
        jnp.sqrt(moment_two / second_fix) + adam_epsilon
    )
    return (params, moment_one, moment_two)

CUTS = ((0, 384), (384, 768), (768, 1152))
ORDERS = ((0, 1, 2), (1, 2, 0), (2, 0, 1))


def coords_of(me):
    return [me // 32, lax.rem(me // 8, 4), lax.rem(me // 2, 4)], lax.rem(me, 2)


def device_of(place, core):
    return place[0] * 32 + place[1] * 8 + place[2] * 2 + core


def moved(place, axis, step):
    return [lax.rem(p + step, 4) if a == axis else p for a, p in enumerate(place)]


def visit_peers(place, core, visit):
    tails = [lax.rem(place[2] + s, 4) * 2 + c for s in range(4) for c in (core, 1 - core)]

    def along_z(i, carry):
        z = lax.rem(place[0] + i, 4) * 32

        def along_x(j, inner):
            base = z + lax.rem(place[1] + j, 4) * 8
            visit([base + tail for tail in tails], i + j > 0)
            return inner

        return lax.fori_loop(0, 4, along_x, carry)

    lax.fori_loop(0, 4, along_z, 0)


def for_peers(place, core, act):
    def visit(others, away):
        pl.when(away)(lambda: act(others[0]))
        for other in others[1:]:
            act(other)

    visit_peers(place, core, visit)


def remote(source, target, send_sem, recv_sem, other):
    return pltpu.make_async_remote_copy(
        src_ref=source,
        dst_ref=target,
        send_sem=send_sem,
        recv_sem=recv_sem,
        device_id=(other,),
        device_id_type=MESH,
    )


def step_kernel(
    rows,
    lists,
    puts,
    ids,
    hot,
    cold_table,
    bias,
    master,
    m_in,
    v_in,
    cot_far,
    down_far,
    up_far,
    cold_m_far,
    cold_v_far,
    out,
    bias_out,
    master_out,
    m_out,
    v_out,
    cold_out,
    cold_m_out,
    cold_v_out,
    *rest,
):
    first, sums0, got1, sums1, got2, sums2, got3 = (rest[3 * i : 3 * i + 3] for i in range(7))
    cot, down, up, cold_m, cold_v, asked, inverse = rest[21:28]
    got, picked, arrived, block, spread_rows, inverse_row = rest[28:34]
    table, x_all, mix_all, grad, pair, part, bias_part = rest[34:41]
    cold, returned, wide, flat, total, bias_sum, bias_got = rest[41:48]
    send_sem, recv_sem, load_sem = rest[48:51]
    list_send, list_recv, row_send, row_recv, cold_send, cold_recv, own_sem = rest[51:]
    f32, bf16 = jnp.float32, jnp.bfloat16
    me = lax.axis_index("dev")
    place, core = coords_of(me)
    partner = device_of(place, 1 - core)
    samples, width = cot.shape
    hot_rows, emb = hot.shape
    count, cap = picked.shape[:2]
    fields = width // emb
    half = down.shape[1]
    dense = 2 * half
    scale = 1.0 / count
    most = pl.ds(0, count - 1)
    nt = (((1,), (1,)), ((), ()))
    tn = (((0,), (0,)), ((), ()))

    barrier = pltpu.get_barrier_semaphore()
    for_peers(
        place,
        core,
        lambda other: pl.semaphore_signal(
            barrier, inc=1, device_id=(other,), device_id_type=MESH
        ),
    )
    loads = [
        pltpu.make_async_copy(far, near, load_sem.at[i])
        for i, (far, near) in enumerate(
            (
                (cot_far, cot),
                (down_far, down),
                (up_far, up),
                (cold_m_far, cold_m),
                (cold_v_far, cold_v),
            )
        )
    ]
    for load in loads:
        load.start()

    which = lax.broadcasted_iota(jnp.int32, (8, samples), 0)
    sample = lax.broadcasted_iota(jnp.int32, (8, samples), 1).astype(f32)

    def invert(t, carry):
        mine = t * 256 + lax.broadcasted_iota(jnp.int32, (256, samples), 0)
        acc = jnp.zeros((8, 256), f32)
        for f in range(fields):
            mask = jnp.where(mine == puts[f : f + 1, :], 1.0, 0.0).astype(bf16)
            code = jnp.where(which == 0, f + 1.0, sample).astype(bf16)
            acc = acc + lax.dot_general(code, mask, nt, preferred_element_type=f32)
        found = ((acc[0:1] - 1.0) * samples + acc[1:2]).astype(jnp.int32)
        inverse_row[:, pl.ds(pl.multiple_of(t * 256, 256), 256)] = jnp.where(
            acc[0:1] > 0.5, jnp.clip(found, 0, fields * samples), fields * samples
        )
        return carry

    lax.fori_loop(0, count * cap // 256, invert, 0)
    pl.semaphore_wait(barrier, count - 1)

    for_peers(
        place,
        core,
        lambda other: remote(lists.at[other], got.at[me], list_send, list_recv, other).start(),
    )
    own = pltpu.make_async_copy(lists.at[me], got.at[me], own_sem)
    own.start()
    own.wait()
    own = pltpu.make_async_copy(inverse_row, inverse, own_sem)
    own.start()
    own.wait()

    def widen_hot(i, carry):
        at = pl.ds(pl.multiple_of(i * 256, 256), 256)
        table[at, :] = hot[at, :].astype(f32)
        return carry

    lax.fori_loop(0, hot_rows // 256, widen_hot, 0)
    all_lists = remote(lists.at[most], got.at[most], list_send, list_recv, partner)
    all_lists.wait_recv()
    read = pltpu.make_async_copy(got, asked, own_sem)
    read.start()
    read.wait()

    def exchange(pick, source, target, sends, receives):
        def send(other):
            remote(source.at[other], target.at[me], sends, receives, other).start()

        def visit(others, away):
            for k, other in enumerate(others):
                pick(other, k)
            pl.when(away)(lambda: send(others[0]))
            for other in others[1:]:
                send(other)

        visit_peers(place, core, visit)
        target[me] = source[me]
        return remote(source.at[most], target.at[most], sends, receives, partner)

    def pick_row(other, k):
        for j in range(cap):
            block[k, pl.ds(j, 1), :] = cold_table[pl.ds(asked[other, 0, j], 1), :]
        picked[other] = block[k].astype(bf16)

    all_rows = exchange(pick_row, picked, arrived, row_send, row_recv)
    turned = got[:, 0, :].astype(f32).T.astype(jnp.int32)
    for j in range(cap):
        spread_rows[:, j * count : (j + 1) * count] = turned[j : j + 1, :]
    grad[pl.ds(fields * samples, 8), :] = jnp.zeros((8, emb), f32)
    for load in loads[:3]:
        load.wait()
    all_rows.wait_recv()

    def widen_cold(i, carry):
        at = pl.ds(pl.multiple_of(hot_rows + i * cap, 8), cap)
        table[at, :] = arrived[i].astype(f32)
        return carry

    lax.fori_loop(0, count, widen_cold, 0)

    def gather_field(f, carry):
        cols = pl.ds(pl.multiple_of(f * emb, emb), emb)

        def gather_rows(i, inner):
            base = pl.multiple_of(f * samples + i * 16, 16)
            for j in range(16):
                grad[pl.ds(base + j, 1), :] = table[pl.ds(rows[base + j], 1), :]
            return inner

        lax.fori_loop(0, samples // 16, gather_rows, 0)
        x = grad[pl.ds(pl.multiple_of(f * samples, samples), samples), :]
        x_all[:, cols] = x.astype(bf16)
        mix_all[:, cols] = (cot[:, cols].astype(f32) * x).astype(bf16)
        return carry

    lax.fori_loop(0, fields, gather_field, 0)
    latent = jnp.dot(x_all[...], down[...], preferred_element_type=f32).astype(bf16)
    back = lax.dot_general(mix_all[...], up[...], nt, preferred_element_type=f32).astype(bf16)
    ones = jnp.ones((8, samples), bf16)

    def per_chunk(n, carry):
        cols = pl.ds(pl.multiple_of(n * 256, 256), 256)
        mixing = jnp.dot(latent, up[:, cols], preferred_element_type=f32) + bias[:, cols]
        from_back = lax.dot_general(back, down[cols, :], nt, preferred_element_type=f32)
        g = cot[:, cols].astype(f32) * (mixing + 1.0) + from_back
        for h in range(2):
            at = pl.ds(pl.multiple_of((2 * n + h) * samples, samples), samples)
            piece = g[:, h * emb : (h + 1) * emb]
            grad[at, :] = piece
            high = piece.astype(bf16)
            pair[at, :emb] = high
            pair[at, emb:] = (piece - high.astype(f32)).astype(bf16)
        z, x = n // 2, pl.ds(lax.rem(n, 2) * 2, 2)
        down_part = lax.dot_general(x_all[:, cols], back, tn, preferred_element_type=f32)
        up_part = lax.dot_general(mix_all[:, cols], latent, tn, preferred_element_type=f32)
        part[z, x, :, :, :, :half] = down_part.astype(bf16).reshape(2, 4, 2, 16, half)
        part[z, x, :, :, :, half:dense] = up_part.astype(bf16).reshape(2, 4, 2, 16, half)
        bias_part[:, cols] = jnp.dot(ones, mix_all[:, cols], preferred_element_type=f32)[:1]
        return carry

    lax.fori_loop(0, width // 256, per_chunk, 0)
    started = []

    def send(src, dst, color, phase, slot, other):
        copy = remote(
            src, dst, send_sem.at[color, phase, slot], recv_sem.at[color, phase, slot], other
        )
        copy.start()
        started.append(copy)
        return copy

    def slab(axis, at, free):
        return tuple(at if a == axis else slice(None) for a in free)

    waiting = {}

    def swap_cores(k):
        low, high = CUTS[k]
        waiting[k] = [
            send(part.at[:, :, :, 1 - core, :, low:high], first[k], k, 0, 0, partner)
        ]

    def collect(k, phase):
        low, high = CUTS[k]
        for copy in waiting[k]:
            copy.wait_recv()
        if phase == 0:

            def add_first(i, carry):
                for x in range(4):
                    mine = part[i, x, :, core, :, low:high].astype(f32)
                    sums0[k][i, x] = (mine + first[k][i, x].astype(f32)).astype(bf16)
                return carry

            lax.fori_loop(0, 4, add_first, 0)
        else:
            before = ORDERS[k][phase - 1]
            free = [a for a in range(3) if a not in ORDERS[k][: phase - 1]]
            source = (sums0, sums1, sums2)[phase - 1][k]
            arrivals = (got1, got2, got3)[phase - 1][k]
            mine = source[slab(before, place[before], free)].astype(f32)
            for slot in range(3):
                mine = mine + arrivals[slot].astype(f32)
            if phase < 3:
                (sums1, sums2)[phase - 1][k][...] = mine.astype(bf16)
            else:
                total[:, low:high] = mine
        if phase < 3:
            axis = ORDERS[k][phase]
            left = [a for a in range(3) if a not in ORDERS[k][:phase]]
            waiting[k] = [
                send(
                    (sums0, sums1, sums2)[phase][k].at[
                        slab(axis, moved(place, axis, s)[axis], left)
                    ],
                    (got1, got2, got3)[phase][k].at[s - 1],
                    k,
                    1 + phase,
                    s - 1,
                    device_of(moved(place, axis, s), core),
                )
                for s in (1, 2, 3)
            ]

    def collect_bias(phase):
        for copy in waiting[3]:
            copy.wait_recv()
        if phase == 0:
            bias_sum[0] = bias_part[...] + bias_got[0, 0]
        else:
            bias_sum[phase] = (bias_sum[phase - 1] + bias_got[phase, 0]) + (
                bias_got[phase, 1] + bias_got[phase, 2]
            )
        if phase < 3:
            waiting[3] = [
                send(
                    bias_sum.at[phase],
                    bias_got.at[phase + 1, s - 1],
                    3,
                    1 + phase,
                    s - 1,
                    device_of(moved(place, phase, s), core),
                )
                for s in (1, 2, 3)
            ]

    swap_cores(0)
    swap_cores(1)
    waiting[3] = [send(bias_part, bias_got.at[0, 0], 3, 0, 0, partner)]

    def pick_grad(other, k):
        base = other * cap
        for j in range(cap):
            block[k, pl.ds(j, 1), :] = grad[pl.ds(inverse[0, base + j], 1), :]
        cold[other] = block[k].astype(bf16)

    all_cold = exchange(pick_grad, cold, returned, cold_send, cold_recv)
    collect(0, 0)
    collect(1, 0)

    def hot_tile(t, carry):
        mine = t * 256 + lax.broadcasted_iota(jnp.int32, (256, samples), 0)
        acc = jnp.zeros((256, 2 * emb), f32)
        for f in range(fields):
            mask = jnp.where(mine == ids[f : f + 1, :], 1.0, 0.0).astype(bf16)
            acc = acc + jnp.dot(
                mask, pair[f * samples : (f + 1) * samples, :], preferred_element_type=f32
            )
        both = (acc[:, :emb] + acc[:, emb:]).astype(bf16)
        x = pl.ds(lax.rem(t, 2) * 2, 2)
        part[t // 2, x, :, :, :, dense:] = both.reshape(2, 4, 2, 16, emb)
        return carry

    lax.fori_loop(0, hot_rows // 256, hot_tile, 0)
    swap_cores(2)
    collect_bias(0)
    collect(2, 0)
    for phase in (1, 2, 3):
        for k in range(3):
            collect(k, phase)
        collect_bias(phase)
    bias_out[...] = bias_sum[3] * scale
    new, m_new, v_new = adam_update(master[...], m_in[...], v_in[...], total[:, :dense] * scale)
    master_out[...] = new
    m_out[...] = m_new
    v_out[...] = v_new
    out[place[0], place[1], place[2], core, :, :dense] = new.astype(bf16)
    out[place[0], place[1], place[2], core, :, dense:] = (total[:, dense:] * scale).astype(bf16)

    def update_cold():
        for load in loads[3:]:
            load.wait()
        all_cold.wait_recv()

        def widen(i, carry):
            wide[pl.ds(pl.multiple_of(i * cap, 8), cap), :] = returned[i].astype(f32)
            return carry

        lax.fori_loop(0, count, widen, 0)
        for j in range(cap):
            flat[j * count : (j + 1) * count, :] = wide[pl.ds(j, count, stride=cap), :].astype(
                bf16
            )

        def update_tile(t, carry):
            at = pl.ds(pl.multiple_of(t * 256, 256), 256)
            mine = t * 256 + lax.broadcasted_iota(jnp.int32, (256, 512), 0)
            acc = jnp.zeros((256, emb), f32)
            for c in range(count * cap // 512):
                cut = slice(c * 512, (c + 1) * 512)
                mask = jnp.where(mine == spread_rows[:, cut], 1.0, 0.0).astype(bf16)
                acc = acc + jnp.dot(mask, flat[cut, :], preferred_element_type=f32)
            new, m_new, v_new = adam_update(
                cold_table[at, :], cold_m[at, :], cold_v[at, :], acc * scale
            )
            cold_out[at, :] = new
            cold_m_out[at, :] = m_new
            cold_v_out[at, :] = v_new
            return carry

        lax.fori_loop(0, cold_table.shape[0] // 256, update_tile, 0)

    for phase in range(4):
        for k, (low, high) in enumerate(CUTS):
            order = ORDERS[k]
            for copy in waiting[k] if phase else []:
                copy.wait_recv()
            spread = order[3 - phase :]
            at = tuple(slice(None) if a in spread else place[a] for a in range(3))
            region = out.at[at + (core, slice(None), slice(low, high))]
            if phase < 3:
                axis = order[2 - phase]
                waiting[k] = [
                    send(
                        region, region, k, 4 + phase, s - 1, device_of(moved(place, axis, s), core)
                    )
                    for s in (1, 2, 3)
                ]
            else:
                waiting[k] = [send(region, region, k, 7, 0, partner)]
        if phase == 2:
            update_cold()
    for k in range(3):
        for copy in waiting[k]:
            copy.wait_recv()
    for copy in started:
        copy.wait_send()
    for everything in (all_lists, all_rows, all_cold):
        everything.wait_send()


def step_all(rows, lists, puts, ids, hot, cold_table, bias, dense_state, cot, down, up, cold_m, cold_v):
    f32, bf16, i32 = jnp.float32, jnp.bfloat16, jnp.int32
    count, cap = lists.shape
    hot_rows, emb = hot.shape
    samples, width = cot.shape
    lookups = samples * width // emb
    total_cols = 2 * down.shape[1] + emb
    widths = [high - low for low, high in CUTS]
    shapes = ((4, 4, 4), (4, 4, 4), (3, 4, 4), (4, 4), (3, 4), (4,), (3,))
    small = jax.ShapeDtypeStruct(dense_state[0].shape, f32)
    slab = jax.ShapeDtypeStruct(cold_table.shape, f32)
    vmem = pl.BlockSpec(memory_space=pltpu.VMEM)
    padded = jnp.pad(lists, ((0, 0), (0, emb - cap))).reshape(count, 1, emb)
    return pl.pallas_call(
        step_kernel,
        out_shape=(
            jax.ShapeDtypeStruct((4, 4, 4, 2, 16, total_cols), bf16),
            jax.ShapeDtypeStruct(bias.shape, f32),
        )
        + (small,) * 3
        + (slab,) * 3,
        in_specs=[pl.BlockSpec(memory_space=pltpu.SMEM)]
        + [vmem] * 9
        + [pl.BlockSpec(memory_space=pl.ANY)] * 5,
        out_specs=(vmem,) * 8,
        scratch_shapes=[
            pltpu.VMEM(shape + (16, cols), bf16) for shape in shapes for cols in widths
        ]
        + [
            pltpu.VMEM(cot.shape, bf16),
            pltpu.VMEM(down.shape, bf16),
            pltpu.VMEM(up.shape, bf16),
            pltpu.VMEM(cold_m.shape, f32),
            pltpu.VMEM(cold_v.shape, f32),
            pltpu.SMEM((count, 1, emb), i32),
            pltpu.SMEM((1, count * cap), i32),
            pltpu.VMEM((count, 1, emb), i32),
            pltpu.VMEM((count, cap, emb), bf16),
            pltpu.VMEM((count, cap, emb), bf16),
            pltpu.VMEM((8, cap, emb), f32),
            pltpu.VMEM((1, count * cap), i32),
            pltpu.VMEM((1, count * cap), i32),
            pltpu.VMEM((hot_rows + count * cap, emb), f32),
            pltpu.VMEM((samples, width), bf16),
            pltpu.VMEM((samples, width), bf16),
            pltpu.VMEM((lookups + 8, emb), f32),
            pltpu.VMEM((lookups, 2 * emb), bf16),
            pltpu.VMEM((4, 4, 4, 2, 16, total_cols), bf16),
            pltpu.VMEM(bias.shape, f32),
            pltpu.VMEM((count, cap, emb), bf16),
            pltpu.VMEM((count, cap, emb), bf16),
            pltpu.VMEM((count * cap + cap, emb), f32),
            pltpu.VMEM((count * cap, emb), bf16),
            pltpu.VMEM((16, total_cols), f32),
            pltpu.VMEM((4,) + bias.shape, f32),
            pltpu.VMEM((4, 3) + bias.shape, f32),
            pltpu.SemaphoreType.DMA((4, 8, 3)),
            pltpu.SemaphoreType.DMA((4, 8, 3)),
            pltpu.SemaphoreType.DMA((5,)),
        ]
        + [pltpu.SemaphoreType.DMA(())] * 7,
        compiler_params=pltpu.CompilerParams(
            collective_id=0, has_side_effects=True, vmem_limit_bytes=60 * 2**20
        ),
        name="step_all",
    )(rows, padded, puts, ids, hot, cold_table, bias, *dense_state, cot, down, up, cold_m, cold_v)


def body(
    cotangent,
    hot_table,
    cold_table,
    cold_m,
    cold_v,
    cross_down,
    cross_up,
    cross_bias,
    dense_master,
    dense_m,
    dense_v,
    hot_ids,
    lookup_slot,
    fetch_rows,
):
    hot_rows = hot_table.shape[0]
    cross_width = cross_down.shape[0]
    is_hot = lookup_slot < 0
    lookup_rows = jnp.where(is_hot, hot_ids, hot_rows + lookup_slot).T.reshape(-1)
    hot_only = jnp.where(is_hot, hot_ids, -1).T
    gathered, bias_grad, master_new, dense_m_new, dense_v_new, cold_new, cold_m_new, cold_v_new = step_all(
        lookup_rows,
        fetch_rows[0],
        lookup_slot.T,
        hot_only,
        hot_table,
        cold_table,
        cross_bias.reshape(1, cross_width),
        (dense_master, dense_m, dense_v),
        cotangent,
        cross_down,
        cross_up,
        cold_m,
        cold_v,
    )
    flat = gathered.reshape(cross_width, -1)
    dense_cols = dense_master.shape[1]
    hot_grad = flat[:, dense_cols:].astype(jnp.float32)
    bias_grad = bias_grad.reshape(cross_width)
    new_weights = flat[:, :dense_cols]
    return (
        hot_grad,
        bias_grad,
        cold_new,
        cold_m_new,
        cold_v_new,
        master_new,
        dense_m_new,
        dense_v_new,
        new_weights,
    )


def solution(mesh):
    return jax.shard_map(
        body,
        mesh=mesh,
        in_specs=(
            P("dev", None),
            P(),
            P("dev", None),
            P("dev", None),
            P("dev", None),
            P(),
            P(),
            P(),
            P("dev", None),
            P("dev", None),
            P("dev", None),
            P("dev", None),
            P("dev", None),
            P("dev", None, None),
        ),
        out_specs=(
            P(),
            P(),
            P("dev", None),
            P("dev", None),
            P("dev", None),
            P("dev", None),
            P("dev", None),
            P("dev", None),
            P(),
        ),
        check_vma=False,
    )
```

time: 445 us -> 126 us (0.28)
  waiting for transfers between devices: 177 us -> 0 us
  Pallas kernels: 0 us -> 109 us
  other arithmetic: 96.2 us -> 3.43 us
  blocking collectives: 67.6 us -> 0 us
  local copies, waits for them, and re-layouts: 51.3 us -> 12.3 us
  starting transfers between devices: 28.7 us -> 0 us
  between operations: 14.3 us -> 0.67 us
  matrix products: 9.81 us -> 0 us
    psum x1 -> x0, waiting for transfers between devices: 160 us -> none  [body(): lax.psum((jnp.concatenate([down_part, up_part], axis=1), hot_part, bias_p...]
    pallas_call x0 -> x1, Pallas kernels: none -> 109 us  [step_all(): pl.pallas_call(step_kernel, out_shape=(jax.ShapeDtypeStruct((4, 4, 4, 2,...]
    psum x1 -> x0, blocking collectives: 67.6 us -> none  [body(): lax.psum((jnp.concatenate([down_part, up_part], axis=1), hot_part, bias_p...]
    scatter-add x3 -> x0, other arithmetic: 65.8 us -> none  [the longest x1 23.9 us: body(): cold_part = jnp.zeros((devices * capacity, emb_width), jnp.float32).at[co...]
    gather x3 -> x0, local copies, waits for them, and re-layouts: 39.6 us -> none  [the longest x1 15 us: body(): jnp.take(hot_table, hot_ids, axis=0)]
    all_to_all x3 -> x0, starting transfers between devices: 28.4 us -> none  [the longest x1 11.5 us: body(): lax.all_to_all(fetch_rows, 'dev', split_axis=1, concat_axis=0, tiled=True)]
    all_to_all x3 -> x0, waiting for transfers between devices: 16.1 us -> none  [the longest x1 16.1 us: body(): lax.all_to_all(picked.reshape(devices, capacity, emb_width), 'dev', split...]
    dot_general x6 -> x0, matrix products: 9.81 us -> none  [the longest x1 2.83 us: body(): lax.dot_general(grad_mix, latent, (((0,), (0,)), ((), ())), preferred_ele...]
  transfers between devices with their start and end apart: 5 -> 0, of which waited for: 2 -> 0; matrix products, arithmetic and copies ran while one was open for 16% -> 0% of each run, Pallas kernels for 0% -> 0%
where the time goes in v4:
time: 126 us; the launch traced here: 125 us
  Pallas kernels  109 us (87%)
  local copies, waits for them, and re-layouts  12.3 us (10%)
  other arithmetic  3.43 us (3%)
    pallas_call x1, Pallas kernels, step_all(): pl.pallas_call(step_kernel, out_shape=(jax.ShapeDtypeStruct((4, 4, 4, 2,...  109 us
    unnamed x23, local copies, waits for them, and re-layouts  6.84 us
    slice x1, local copies, waits for them, and re-layouts, body(): new_weights = flat[:, :dense_cols]  4.79 us

profile of v4, /device:TPU:1, one launch (start us, length us, event | category | flops | bytes accessed | tf_op | source)
XLA Modules:
  0.0 125.2 jit_solution(12259264110207552208)
XLA Ops:
  0.6 1.3 %select_bitcast_fusion = (s32[16,256]{1,0:T(8,128)}, s32[2,2,8,128]{3,2,1,0:T(8,128)S(1)}) fusion(s32[256,16]{0,1:T(8,128)} %param.25, s32[256,16]{0,1:T(8,128)} %param.26), kind=kLoop, calls=%fused_computation.1 | loop fusion | flops 16384 | bytes 65536 | tf_op jit(solution)/shard_map/transpose | solution.py:547
  2.0 0.6 copy.24
  2.6 0.8 copy.23
  3.4 0.6 pad.4
  4.0 108.9 %step_all.1 = (bf16[4,4,4,2,16,1152]{5,4,3,2,1,0:T(8,128)(2,1)}, f32[1,2048]{1,0:T(1,128)}, f32[16,1024]{1,0:T(8,128)}, f32[16,1024]{1,0:T(8,128)}, f32[16,1024]...) custom-call(s32[4096]{0:T(1024)} %bitcast.16, s32[128,1,128]{2,1,0:T(1,128)} %bitcast.14, ...), custom_call_target="tpu_custom_call" | custom-call | tf_op jit(solution)/shard_map/step_all/pallas_call | solution.py:472
  112.9 2.1 %slice_convert_fusion = f32[2048,128]{1,0:T(8,128)} fusion(bf16[2048,1152]{1,0:T(8,128)(2,1)} %bitcast.12), kind=kLoop, calls=%fused_computation | loop fusion | flops 262144 | bytes 1572864 | tf_op jit(solution)/shard_map/convert_element_type | solution.py:565
  115.0 0.0 copy-start.6
  115.0 0.0 copy-start.2
  115.0 0.0 copy-start.1
  115.0 4.8 %slice.9 = bf16[2048,1024]{1,0:T(8,128)(2,1)} slice(bf16[2048,1152]{1,0:T(8,128)(2,1)} %bitcast.13), slice={[0:2048], [0:1024]} | slice | bytes 8388608 | tf_op jit(solution)/shard_map/slice | solution.py:567
  119.8 0.0 copy-done.6
  119.8 0.0 copy-start
  119.8 0.0 copy-start.5
  119.8 0.0 copy-start.4
  119.8 0.0 copy-start.3
  119.8 0.6 copy.32
  120.4 0.0 copy-done.2
  120.4 1.0 copy.33
  121.4 0.0 copy-done.1
  121.4 1.0 copy.34
  122.4 0.0 copy-done
  122.4 1.0 copy.35
  123.3 0.0 copy-done.5
  123.4 0.6 copy.36
  124.0 0.0 copy-done.4
  124.0 0.6 copy.37
  124.6 0.0 copy-done.3
  124.6 0.6 copy.38
Async XLA Ops:
  115.0 4.8 %copy-start.6 = (f32[1,2048]{1,0:T(1,128)S(1)}, f32[1,2048]{1,0:T(1,128)}, u32[]{:S(2)}) copy-start(f32[1,2048]{1,0:T(1,128)} %get-tuple-element.18) | copy-start | bytes 24580
  115.0 5.4 %copy-start.2 = (f32[2048,128]{1,0:T(8,128)S(1)}, f32[2048,128]{1,0:T(8,128)}, u32[]{:S(2)}) copy-start(f32[2048,128]{1,0:T(8,128)} %get-tuple-element.38) | copy-start | bytes 3145732
  115.0 6.4 %copy-start.1 = (f32[2048,128]{1,0:T(8,128)S(1)}, f32[2048,128]{1,0:T(8,128)}, u32[]{:S(2)}) copy-start(f32[2048,128]{1,0:T(8,128)} %get-tuple-element.39) | copy-start | bytes 3145732
  119.8 2.6 %copy-start = (f32[2048,128]{1,0:T(8,128)S(1)}, f32[2048,128]{1,0:T(8,128)}, u32[]{:S(2)}) copy-start(f32[2048,128]{1,0:T(8,128)} %get-tuple-element.40) | copy-start | bytes 3145732
  119.8 3.5 %copy-start.5 = (f32[16,1024]{1,0:T(8,128)S(1)}, f32[16,1024]{1,0:T(8,128)}, u32[]{:S(2)}) copy-start(f32[16,1024]{1,0:T(8,128)} %get-tuple-element.41) | copy-start | bytes 196612
  119.8 4.2 %copy-start.4 = (f32[16,1024]{1,0:T(8,128)S(1)}, f32[16,1024]{1,0:T(8,128)}, u32[]{:S(2)}) copy-start(f32[16,1024]{1,0:T(8,128)} %get-tuple-element.42) | copy-start | bytes 196612
  119.8 4.8 %copy-start.3 = (f32[16,1024]{1,0:T(8,128)S(1)}, f32[16,1024]{1,0:T(8,128)}, u32[]{:S(2)}) copy-start(f32[16,1024]{1,0:T(8,128)} %get-tuple-element.43) | copy-start | bytes 196612

commit v5 on v4

--- a/solution.py
+++ b/solution.py
@@ -23,8 +23,10 @@
     )
     return (params, moment_one, moment_two)
 
-CUTS = ((0, 384), (384, 768), (768, 1152))
-ORDERS = ((0, 1, 2), (1, 2, 0), (2, 0, 1))
+CUTS = ((0, 384), (384, 768), (768, 1024), (1024, 1152))
+ORDERS = ((0, 1, 2), (1, 2, 0), (2, 0, 1), (2, 0, 1))
+COLORS = len(CUTS)
+BIAS = COLORS
 
 
 def coords_of(me):
@@ -93,21 +95,24 @@
     cold_v_far,
     out,
     bias_out,
-    master_out,
-    m_out,
-    v_out,
+    total_out,
     cold_out,
     cold_m_out,
     cold_v_out,
     *rest,
 ):
-    first, sums0, got1, sums1, got2, sums2, got3 = (rest[3 * i : 3 * i + 3] for i in range(7))
+    first, sums0, got1, sums1, got2, sums2, got3 = (
+        rest[COLORS * i : COLORS * i + COLORS] for i in range(7)
+    )
+    rest = rest[COLORS * 7 - 21 :]
     cot, down, up, cold_m, cold_v, asked, inverse = rest[21:28]
     got, picked, arrived, block, spread_rows, inverse_row = rest[28:34]
     table, x_all, mix_all, grad, pair, part, bias_part = rest[34:41]
     cold, returned, wide, flat, total, bias_sum, bias_got = rest[41:48]
+    mid = rest[58]
+    stage_send, stage_recv, far_sem = rest[59:]
     send_sem, recv_sem, load_sem = rest[48:51]
-    list_send, list_recv, row_send, row_recv, cold_send, cold_recv, own_sem = rest[51:]
+    list_send, list_recv, row_send, row_recv, cold_send, cold_recv, own_sem = rest[51:58]
     f32, bf16 = jnp.float32, jnp.bfloat16
     me = lax.axis_index("dev")
     place, core = coords_of(me)
@@ -123,14 +128,22 @@
     nt = (((1,), (1,)), ((), ()))
     tn = (((0,), (0,)), ((), ()))
 
+    plane, spot = place[0] * 4 + place[1], place[2] * 2 + core
+    planes = [
+        lax.rem(place[0] + i, 4) * 4 + lax.rem(place[1] + j, 4)
+        for i in range(4)
+        for j in range(4)
+        if i + j > 0
+    ]
+    spots = [
+        lax.rem(place[2] + i, 4) * 2 + c
+        for i in range(4)
+        for c in (core, 1 - core)
+    ][1:]
     barrier = pltpu.get_barrier_semaphore()
-    for_peers(
-        place,
-        core,
-        lambda other: pl.semaphore_signal(
-            barrier, inc=1, device_id=(other,), device_id_type=MESH
-        ),
-    )
+    greeted = [other * 8 + spot for other in planes] + [plane * 8 + other for other in spots]
+    for other in greeted:
+        pl.semaphore_signal(barrier, inc=1, device_id=(other,), device_id_type=MESH)
     loads = [
         pltpu.make_async_copy(far, near, load_sem.at[i])
         for i, (far, near) in enumerate(
@@ -162,20 +175,13 @@
         )
         return carry
 
+    mid[plane] = lists[plane]
     lax.fori_loop(0, count * cap // 256, invert, 0)
-    pl.semaphore_wait(barrier, count - 1)
-
-    for_peers(
-        place,
-        core,
-        lambda other: remote(lists.at[other], got.at[me], list_send, list_recv, other).start(),
-    )
-    own = pltpu.make_async_copy(lists.at[me], got.at[me], own_sem)
-    own.start()
-    own.wait()
-    own = pltpu.make_async_copy(inverse_row, inverse, own_sem)
-    own.start()
-    own.wait()
+    keep = pltpu.make_async_copy(inverse_row, inverse, own_sem)
+    keep.start()
+    pl.semaphore_wait(barrier, len(greeted))
+    for other in planes:
+        remote(lists.at[other], mid.at[plane], list_send, list_recv, other * 8 + spot).start()
 
     def widen_hot(i, carry):
         at = pl.ds(pl.multiple_of(i * 256, 256), 256)
@@ -183,9 +189,18 @@
         return carry
 
     lax.fori_loop(0, hot_rows // 256, widen_hot, 0)
-    all_lists = remote(lists.at[most], got.at[most], list_send, list_recv, partner)
+    part_of = pl.ds(0, len(planes))
+    all_lists = remote(lists.at[part_of], mid.at[part_of], list_send, list_recv, partner)
     all_lists.wait_recv()
-    read = pltpu.make_async_copy(got, asked, own_sem)
+    for other in spots:
+        remote(
+            mid.at[:, other], got.at[:, spot], stage_send, stage_recv, plane * 8 + other
+        ).start()
+    got[:, spot] = mid[:, spot]
+    part_of = pl.ds(0, len(spots))
+    all_stage = remote(mid.at[:, part_of], got.at[:, part_of], stage_send, stage_recv, partner)
+    all_stage.wait_recv()
+    read = pltpu.make_async_copy(got, asked, far_sem)
     read.start()
     read.wait()
 
@@ -206,11 +221,11 @@
 
     def pick_row(other, k):
         for j in range(cap):
-            block[k, pl.ds(j, 1), :] = cold_table[pl.ds(asked[other, 0, j], 1), :]
+            block[k, pl.ds(j, 1), :] = cold_table[pl.ds(asked[other // 8, lax.rem(other, 8), 0, j], 1), :]
         picked[other] = block[k].astype(bf16)
 
     all_rows = exchange(pick_row, picked, arrived, row_send, row_recv)
-    turned = got[:, 0, :].astype(f32).T.astype(jnp.int32)
+    turned = got[:, :, 0, :].reshape(count, emb).astype(f32).T.astype(jnp.int32)
     for j in range(cap):
         spread_rows[:, j * count : (j + 1) * count] = turned[j : j + 1, :]
     grad[pl.ds(fields * samples, 8), :] = jnp.zeros((8, emb), f32)
@@ -245,7 +260,17 @@
     back = lax.dot_general(mix_all[...], up[...], nt, preferred_element_type=f32).astype(bf16)
     ones = jnp.ones((8, samples), bf16)
 
-    def per_chunk(n, carry):
+    def weight_chunk(n, carry):
+        cols = pl.ds(pl.multiple_of(n * 256, 256), 256)
+        z, x = n // 2, pl.ds(lax.rem(n, 2) * 2, 2)
+        down_part = lax.dot_general(x_all[:, cols], back, tn, preferred_element_type=f32)
+        up_part = lax.dot_general(mix_all[:, cols], latent, tn, preferred_element_type=f32)
+        part[z, x, :, :, :, :half] = down_part.astype(bf16).reshape(2, 4, 2, 16, half)
+        part[z, x, :, :, :, half:dense] = up_part.astype(bf16).reshape(2, 4, 2, 16, half)
+        bias_part[:, cols] = jnp.dot(ones, mix_all[:, cols], preferred_element_type=f32)[:1]
+        return carry
+
+    def grad_chunk(n, carry):
         cols = pl.ds(pl.multiple_of(n * 256, 256), 256)
         mixing = jnp.dot(latent, up[:, cols], preferred_element_type=f32) + bias[:, cols]
         from_back = lax.dot_general(back, down[cols, :], nt, preferred_element_type=f32)
@@ -257,15 +282,9 @@
             high = piece.astype(bf16)
             pair[at, :emb] = high
             pair[at, emb:] = (piece - high.astype(f32)).astype(bf16)
-        z, x = n // 2, pl.ds(lax.rem(n, 2) * 2, 2)
-        down_part = lax.dot_general(x_all[:, cols], back, tn, preferred_element_type=f32)
-        up_part = lax.dot_general(mix_all[:, cols], latent, tn, preferred_element_type=f32)
-        part[z, x, :, :, :, :half] = down_part.astype(bf16).reshape(2, 4, 2, 16, half)
-        part[z, x, :, :, :, half:dense] = up_part.astype(bf16).reshape(2, 4, 2, 16, half)
-        bias_part[:, cols] = jnp.dot(ones, mix_all[:, cols], preferred_element_type=f32)[:1]
         return carry
 
-    lax.fori_loop(0, width // 256, per_chunk, 0)
+    lax.fori_loop(0, width // 256, weight_chunk, 0)
     started = []
 
     def send(src, dst, color, phase, slot, other):
@@ -330,7 +349,7 @@
             ]
 
     def collect_bias(phase):
-        for copy in waiting[3]:
+        for copy in waiting[BIAS]:
             copy.wait_recv()
         if phase == 0:
             bias_sum[0] = bias_part[...] + bias_got[0, 0]
@@ -339,11 +358,11 @@
                 bias_got[phase, 1] + bias_got[phase, 2]
             )
         if phase < 3:
-            waiting[3] = [
+            waiting[BIAS] = [
                 send(
                     bias_sum.at[phase],
                     bias_got.at[phase + 1, s - 1],
-                    3,
+                    BIAS,
                     1 + phase,
                     s - 1,
                     device_of(moved(place, phase, s), core),
@@ -351,19 +370,19 @@
                 for s in (1, 2, 3)
             ]
 
-    swap_cores(0)
-    swap_cores(1)
-    waiting[3] = [send(bias_part, bias_got.at[0, 0], 3, 0, 0, partner)]
+    for k in range(3):
+        swap_cores(k)
+    waiting[BIAS] = [send(bias_part, bias_got.at[0, 0], BIAS, 0, 0, partner)]
+    lax.fori_loop(0, width // 256, grad_chunk, 0)
+    for k in range(3):
+        collect(k, 0)
+    collect_bias(0)
 
     def pick_grad(other, k):
         base = other * cap
         for j in range(cap):
             block[k, pl.ds(j, 1), :] = grad[pl.ds(inverse[0, base + j], 1), :]
         cold[other] = block[k].astype(bf16)
-
-    all_cold = exchange(pick_grad, cold, returned, cold_send, cold_recv)
-    collect(0, 0)
-    collect(1, 0)
 
     def hot_tile(t, carry):
         mine = t * 256 + lax.broadcasted_iota(jnp.int32, (256, samples), 0)
@@ -379,18 +398,17 @@
         return carry
 
     lax.fori_loop(0, hot_rows // 256, hot_tile, 0)
-    swap_cores(2)
-    collect_bias(0)
-    collect(2, 0)
+    swap_cores(3)
+    keep.wait()
+    all_cold = exchange(pick_grad, cold, returned, cold_send, cold_recv)
+    collect(3, 0)
     for phase in (1, 2, 3):
-        for k in range(3):
+        for k in range(COLORS):
             collect(k, phase)
         collect_bias(phase)
     bias_out[...] = bias_sum[3] * scale
-    new, m_new, v_new = adam_update(master[...], m_in[...], v_in[...], total[:, :dense] * scale)
-    master_out[...] = new
-    m_out[...] = m_new
-    v_out[...] = v_new
+    new = adam_update(master[...], m_in[...], v_in[...], total[:, :dense] * scale)[0]
+    total_out[...] = total[:, :dense]
     out[place[0], place[1], place[2], core, :, :dense] = new.astype(bf16)
     out[place[0], place[1], place[2], core, :, dense:] = (total[:, dense:] * scale).astype(bf16)
 
@@ -447,12 +465,12 @@
                 waiting[k] = [send(region, region, k, 7, 0, partner)]
         if phase == 2:
             update_cold()
-    for k in range(3):
+    for k in range(COLORS):
         for copy in waiting[k]:
             copy.wait_recv()
     for copy in started:
         copy.wait_send()
-    for everything in (all_lists, all_rows, all_cold):
+    for everything in (all_lists, all_stage, all_rows, all_cold):
         everything.wait_send()
 
 
@@ -468,19 +486,19 @@
     small = jax.ShapeDtypeStruct(dense_state[0].shape, f32)
     slab = jax.ShapeDtypeStruct(cold_table.shape, f32)
     vmem = pl.BlockSpec(memory_space=pltpu.VMEM)
-    padded = jnp.pad(lists, ((0, 0), (0, emb - cap))).reshape(count, 1, emb)
+    padded = jnp.pad(lists, ((0, 0), (0, emb - cap))).reshape(16, 8, 1, emb)
     return pl.pallas_call(
         step_kernel,
         out_shape=(
             jax.ShapeDtypeStruct((4, 4, 4, 2, 16, total_cols), bf16),
             jax.ShapeDtypeStruct(bias.shape, f32),
         )
-        + (small,) * 3
+        + (small,)
         + (slab,) * 3,
         in_specs=[pl.BlockSpec(memory_space=pltpu.SMEM)]
         + [vmem] * 9
         + [pl.BlockSpec(memory_space=pl.ANY)] * 5,
-        out_specs=(vmem,) * 8,
+        out_specs=(vmem,) * 6,
         scratch_shapes=[
             pltpu.VMEM(shape + (16, cols), bf16) for shape in shapes for cols in widths
         ]
@@ -490,9 +508,9 @@
             pltpu.VMEM(up.shape, bf16),
             pltpu.VMEM(cold_m.shape, f32),
             pltpu.VMEM(cold_v.shape, f32),
-            pltpu.SMEM((count, 1, emb), i32),
+            pltpu.SMEM((16, 8, 1, emb), i32),
             pltpu.SMEM((1, count * cap), i32),
-            pltpu.VMEM((count, 1, emb), i32),
+            pltpu.VMEM((16, 8, 1, emb), i32),
             pltpu.VMEM((count, cap, emb), bf16),
             pltpu.VMEM((count, cap, emb), bf16),
             pltpu.VMEM((8, cap, emb), f32),
@@ -512,13 +530,15 @@
             pltpu.VMEM((16, total_cols), f32),
             pltpu.VMEM((4,) + bias.shape, f32),
             pltpu.VMEM((4, 3) + bias.shape, f32),
-            pltpu.SemaphoreType.DMA((4, 8, 3)),
-            pltpu.SemaphoreType.DMA((4, 8, 3)),
+            pltpu.SemaphoreType.DMA((COLORS + 1, 8, 3)),
+            pltpu.SemaphoreType.DMA((COLORS + 1, 8, 3)),
             pltpu.SemaphoreType.DMA((5,)),
         ]
-        + [pltpu.SemaphoreType.DMA(())] * 7,
+        + [pltpu.SemaphoreType.DMA(())] * 7
+        + [pltpu.VMEM((16, 8, 1, emb), i32)]
+        + [pltpu.SemaphoreType.DMA(())] * 3,
         compiler_params=pltpu.CompilerParams(
-            collective_id=0, has_side_effects=True, vmem_limit_bytes=60 * 2**20
+            collective_id=0, has_side_effects=True, vmem_limit_bytes=48 * 2**20
         ),
         name="step_all",
     )(rows, padded, puts, ids, hot, cold_table, bias, *dense_state, cot, down, up, cold_m, cold_v)
@@ -545,7 +565,7 @@
     is_hot = lookup_slot < 0
     lookup_rows = jnp.where(is_hot, hot_ids, hot_rows + lookup_slot).T.reshape(-1)
     hot_only = jnp.where(is_hot, hot_ids, -1).T
-    gathered, bias_grad, master_new, dense_m_new, dense_v_new, cold_new, cold_m_new, cold_v_new = step_all(
+    gathered, bias_grad, total, cold_new, cold_m_new, cold_v_new = step_all(
         lookup_rows,
         fetch_rows[0],
         lookup_slot.T,
@@ -562,6 +582,9 @@
     )
     flat = gathered.reshape(cross_width, -1)
     dense_cols = dense_master.shape[1]
+    master_new, dense_m_new, dense_v_new = adam_update(
+        dense_master, dense_m, dense_v, total * (1.0 / lax.axis_size("dev"))
+    )
     hot_grad = flat[:, dense_cols:].astype(jnp.float32)
     bias_grad = bias_grad.reshape(cross_width)
     new_weights = flat[:, :dense_cols]

time: 126 us -> 131 us (1.040)
  local copies, waits for them, and re-layouts: 12.3 us -> 16.4 us
    unnamed x23 -> x22, local copies, waits for them, and re-layouts: 6.84 us -> 11.7 us
where the time goes in v5:
time: 131 us
  Pallas kernels  110 us (84%)
  local copies, waits for them, and re-layouts  16.4 us (13%)
  other arithmetic  3.51 us (3%)
    pallas_call x1, Pallas kernels, step_all(): pl.pallas_call(step_kernel, out_shape=(jax.ShapeDtypeStruct((4, 4, 4, 2,...  110 us
    unnamed x22, local copies, waits for them, and re-layouts  11.7 us
    slice x1, local copies, waits for them, and re-layouts, body(): new_weights = flat[:, :dense_cols]  4.64 us

profile of v5, /device:TPU:1, one launch (start us, length us, event | category | flops | bytes accessed | tf_op | source)
XLA Modules:
  0.0 130.5 jit_solution(14780723542702362403)
XLA Ops:
  0.6 0.7 select_bitcast_fusion
  1.4 0.8 copy.24
  2.2 0.0 copy-start
  2.2 1.2 copy-done
  3.4 0.0 copy-start.1
  3.4 1.2 copy-done.1
  4.7 0.0 copy-start.2
  4.7 1.0 copy-done.2
  5.7 0.0 copy-start.3
  5.7 0.8 copy-done.3
  6.6 0.0 copy-start.4
  6.6 0.8 copy-done.4
  7.4 0.0 copy-start.5
  7.4 0.8 copy-done.5
  8.2 0.0 copy-start.6
  8.2 0.7 copy-done.6
  9.0 0.0 copy-start.7
  9.0 0.7 copy-done.7
  9.6 109.9 %step_all.1 = (bf16[4,4,4,2,16,1152]{5,4,3,2,1,0:T(8,128)(2,1)}, f32[1,2048]{1,0:T(1,128)S(1)}, f32[16,1024]{1,0:T(8,128)S(1)}, f32[2048,128]{1,0:T(8,128)S(1)},...) custom-call(s32[4096]{0:T(1024)S(1)} %bitcast.13, s32[16,8,1,128]{3,2,1,0:T(1,128)S(1)} %bitcast.12, ...), custom_call_target="tpu_custom_call" | custom-call | tf_op jit(solution)/shard_map/step_all/pallas_call | solution.py:490
  119.6 0.7 divide_subtract_fusion
  120.3 2.1 %slice_convert_fusion = f32[2048,128]{1,0:T(8,128)} fusion(bf16[2048,1152]{1,0:T(8,128)(2,1)} %bitcast.17), kind=kLoop, calls=%fused_computation | loop fusion | flops 262144 | bytes 1572864 | tf_op jit(solution)/shard_map/convert_element_type | solution.py:588
  122.4 4.6 %slice.9 = bf16[2048,1024]{1,0:T(8,128)(2,1)} slice(bf16[2048,1152]{1,0:T(8,128)(2,1)} %bitcast.18), slice={[0:2048], [0:1024]} | slice | bytes 8388608 | tf_op jit(solution)/shard_map/slice | solution.py:590
  127.0 0.6 copy.30
  127.6 1.0 copy.31
  128.6 1.0 copy.32
  129.5 1.0 copy.33
  (2 shorter events, 0.0 us)
Async XLA Ops:
  2.2 1.2 copy-start
  3.4 1.2 copy-start.1
  4.7 1.0 copy-start.2
  5.7 0.8 copy-start.3
  6.6 0.8 copy-start.4
  7.4 0.8 copy-start.5
  8.2 0.7 copy-start.6
  9.0 0.7 copy-start.7

commit v6 on v5

--- a/solution.py
+++ b/solution.py
@@ -93,7 +93,8 @@
     up_far,
     cold_m_far,
     cold_v_far,
-    out,
+    dense_out,
+    hot_out,
     bias_out,
     total_out,
     cold_out,
@@ -176,9 +177,6 @@
         return carry
 
     mid[plane] = lists[plane]
-    lax.fori_loop(0, count * cap // 256, invert, 0)
-    keep = pltpu.make_async_copy(inverse_row, inverse, own_sem)
-    keep.start()
     pl.semaphore_wait(barrier, len(greeted))
     for other in planes:
         remote(lists.at[other], mid.at[plane], list_send, list_recv, other * 8 + spot).start()
@@ -200,7 +198,11 @@
     part_of = pl.ds(0, len(spots))
     all_stage = remote(mid.at[:, part_of], got.at[:, part_of], stage_send, stage_recv, partner)
     all_stage.wait_recv()
-    read = pltpu.make_async_copy(got, asked, far_sem)
+    turned = got[:, :, 0, :].reshape(count, emb).astype(f32).T.astype(jnp.int32)
+    turned = jnp.clip(turned, 0, cold_table.shape[0] - 1)
+    for j in range(cap):
+        spread_rows[:, j * count : (j + 1) * count] = turned[j : j + 1, :]
+    read = pltpu.make_async_copy(spread_rows, asked, far_sem)
     read.start()
     read.wait()
 
@@ -221,13 +223,13 @@
 
     def pick_row(other, k):
         for j in range(cap):
-            block[k, pl.ds(j, 1), :] = cold_table[pl.ds(asked[other // 8, lax.rem(other, 8), 0, j], 1), :]
+            block[k, pl.ds(j, 1), :] = cold_table[pl.ds(asked[0, j * count + other], 1), :]
         picked[other] = block[k].astype(bf16)
 
     all_rows = exchange(pick_row, picked, arrived, row_send, row_recv)
-    turned = got[:, :, 0, :].reshape(count, emb).astype(f32).T.astype(jnp.int32)
-    for j in range(cap):
-        spread_rows[:, j * count : (j + 1) * count] = turned[j : j + 1, :]
+    lax.fori_loop(0, count * cap // 256, invert, 0)
+    keep = pltpu.make_async_copy(inverse_row, inverse, own_sem)
+    keep.start()
     grad[pl.ds(fields * samples, 8), :] = jnp.zeros((8, emb), f32)
     for load in loads[:3]:
         load.wait()
@@ -409,8 +411,9 @@
     bias_out[...] = bias_sum[3] * scale
     new = adam_update(master[...], m_in[...], v_in[...], total[:, :dense] * scale)[0]
     total_out[...] = total[:, :dense]
-    out[place[0], place[1], place[2], core, :, :dense] = new.astype(bf16)
-    out[place[0], place[1], place[2], core, :, dense:] = (total[:, dense:] * scale).astype(bf16)
+    at = (place[0], place[1], place[2], core)
+    dense_out[at] = new.astype(bf16)
+    hot_out[at] = (total[:, dense:] * scale).astype(bf16)
 
     def update_cold():
         for load in loads[3:]:
@@ -452,7 +455,8 @@
                 copy.wait_recv()
             spread = order[3 - phase :]
             at = tuple(slice(None) if a in spread else place[a] for a in range(3))
-            region = out.at[at + (core, slice(None), slice(low, high))]
+            at = at + (core, slice(None))
+            region = dense_out.at[at + (slice(low, high),)] if high <= dense else hot_out.at[at]
             if phase < 3:
                 axis = order[2 - phase]
                 waiting[k] = [
@@ -490,7 +494,8 @@
     return pl.pallas_call(
         step_kernel,
         out_shape=(
-            jax.ShapeDtypeStruct((4, 4, 4, 2, 16, total_cols), bf16),
+            jax.ShapeDtypeStruct((4, 4, 4, 2, 16, total_cols - emb), bf16),
+            jax.ShapeDtypeStruct((4, 4, 4, 2, 16, emb), bf16),
             jax.ShapeDtypeStruct(bias.shape, f32),
         )
         + (small,)
@@ -498,7 +503,7 @@
         in_specs=[pl.BlockSpec(memory_space=pltpu.SMEM)]
         + [vmem] * 9
         + [pl.BlockSpec(memory_space=pl.ANY)] * 5,
-        out_specs=(vmem,) * 6,
+        out_specs=(vmem,) * 7,
         scratch_shapes=[
             pltpu.VMEM(shape + (16, cols), bf16) for shape in shapes for cols in widths
         ]
@@ -508,7 +513,7 @@
             pltpu.VMEM(up.shape, bf16),
             pltpu.VMEM(cold_m.shape, f32),
             pltpu.VMEM(cold_v.shape, f32),
-            pltpu.SMEM((16, 8, 1, emb), i32),
+            pltpu.SMEM((1, count * cap), i32),
             pltpu.SMEM((1, count * cap), i32),
             pltpu.VMEM((16, 8, 1, emb), i32),
             pltpu.VMEM((count, cap, emb), bf16),
@@ -538,7 +543,7 @@
         + [pltpu.VMEM((16, 8, 1, emb), i32)]
         + [pltpu.SemaphoreType.DMA(())] * 3,
         compiler_params=pltpu.CompilerParams(
-            collective_id=0, has_side_effects=True, vmem_limit_bytes=48 * 2**20
+            collective_id=0, has_side_effects=True, vmem_limit_bytes=60 * 2**20
         ),
         name="step_all",
     )(rows, padded, puts, ids, hot, cold_table, bias, *dense_state, cot, down, up, cold_m, cold_v)
@@ -565,7 +570,7 @@
     is_hot = lookup_slot < 0
     lookup_rows = jnp.where(is_hot, hot_ids, hot_rows + lookup_slot).T.reshape(-1)
     hot_only = jnp.where(is_hot, hot_ids, -1).T
-    gathered, bias_grad, total, cold_new, cold_m_new, cold_v_new = step_all(
+    new_weights, hot_grad, bias_grad, total, cold_new, cold_m_new, cold_v_new = step_all(
         lookup_rows,
         fetch_rows[0],
         lookup_slot.T,
@@ -580,14 +585,12 @@
         cold_m,
         cold_v,
     )
-    flat = gathered.reshape(cross_width, -1)
-    dense_cols = dense_master.shape[1]
     master_new, dense_m_new, dense_v_new = adam_update(
         dense_master, dense_m, dense_v, total * (1.0 / lax.axis_size("dev"))
     )
-    hot_grad = flat[:, dense_cols:].astype(jnp.float32)
+    hot_grad = hot_grad.reshape(hot_table.shape).astype(jnp.float32)
     bias_grad = bias_grad.reshape(cross_width)
-    new_weights = flat[:, :dense_cols]
+    new_weights = new_weights.reshape(cross_width, -1)
     return (
         hot_grad,
         bias_grad,

time: 131 us -> 121 us (0.924)
  Pallas kernels: 110 us -> 104 us
  local copies, waits for them, and re-layouts: 16.4 us -> 10.9 us
  other arithmetic: 3.51 us -> 5.11 us
    pallas_call x1, Pallas kernels: 110 us -> 104 us  [step_all(): pl.pallas_call(step_kernel, out_shape=(jax.ShapeDtypeStruct((4, 4, 4, 2,...]
    slice x1 -> x0, local copies, waits for them, and re-layouts: 4.64 us -> none  [body(): new_weights = flat[:, :dense_cols]]
    unnamed x22 -> x17, local copies, waits for them, and re-layouts: 11.7 us -> 10.2 us
where the time goes in v6:
time: 121 us; the launch traced here: 120 us
  Pallas kernels  104 us (86%)
  local copies, waits for them, and re-layouts  10.9 us (9%)
  other arithmetic  5.11 us (4%)
    pallas_call x1, Pallas kernels, step_all(): pl.pallas_call(step_kernel, out_shape=(jax.ShapeDtypeStruct((4, 4, 4, 2,...  104 us
    unnamed x17, local copies, waits for them, and re-layouts  10.2 us

profile of v6, /device:TPU:1, one launch (start us, length us, event | category | flops | bytes accessed | tf_op | source)
XLA Modules:
  0.0 120.3 jit_solution(18187198119777405247)
XLA Ops:
  0.6 1.3 %select_bitcast_fusion = (s32[16,256]{1,0:T(8,128)}, s32[2,2,8,128]{3,2,1,0:T(8,128)S(1)}) fusion(s32[256,16]{0,1:T(8,128)} %param.25, s32[256,16]{0,1:T(8,128)} %param.26), kind=kLoop, calls=%fused_computation.4 | loop fusion | flops 16384 | bytes 65536 | tf_op jit(solution)/shard_map/transpose | solution.py:572
  2.0 0.6 copy.25
  2.6 0.8 copy.24
  3.4 0.6 pad.4.clone
  4.0 0.0 copy-start.2
  4.0 0.0 copy-start.3
  4.0 0.0 copy-start.4
  4.1 103.6 %step_all.1 = (bf16[4,4,4,2,16,1024]{5,4,3,2,1,0:T(8,128)(2,1)}, bf16[4,4,4,2,16,128]{5,4,3,2,1,0:T(8,128)(2,1)}, f32[1,2048]{1,0:T(1,128)}, f32[16,1024]{1,0:T(...) custom-call(s32[4096]{0:T(1024)} %bitcast.17, s32[16,8,1,128]{3,2,1,0:T(1,128)} %bitcast.16, ...), custom_call_target="tpu_custom_call" | custom-call | tf_op jit(solution)/shard_map/step_all/pallas_call | solution.py:494
  107.6 0.0 copy-start.1
  107.6 0.0 copy-start
  107.7 0.0 copy-done.2
  107.7 0.0 copy-done.3
  107.7 0.0 copy-done.4
  107.7 1.7 %divide_subtract_fusion = (f32[16,1024]{1,0:T(8,128)}, f32[16,1024]{1,0:T(8,128)}, f32[16,1024]{1,0:T(8,128)}) fusion(f32[16,1024]{1,0:T(8,128)S(1)} %copy-done.2, f32[16,1024]{1,0:T(8,128)} %get-tuple-element.21, f32[16,1024]{1,0:T(8,128)S(1)} %copy-done.3, f32[16,1024]{1,0:T(8,128)S(1)} %copy-done.4), kind=kLoop, calls=%fused_computation.1 | loop fusion | flops 212992 | bytes 458752 | tf_op jit(solution)/shard_map/sub | solution.py:21
  109.4 2.1 %bitcast_convert_fusion = f32[2048,128]{1,0:T(8,128)} fusion(bf16[4,4,4,2,16,128]{5,4,3,2,1,0:T(8,128)(2,1)} %get-tuple-element.16), kind=kLoop, calls=%fused_computation | loop fusion | flops 262144 | bytes 1572864 | tf_op jit(solution)/shard_map/convert_element_type | solution.py:591
  111.4 1.3 %copy.31 = f32[2048]{0:T(1024)} copy(f32[2048]{0:T(1024)} %bitcast.20) | data formatting | bytes 16384
  112.7 2.3 %copy.32 = f32[2048,128]{1,0:T(8,128)} copy(f32[2048,128]{1,0:T(8,128)} %get-tuple-element.39) | data formatting | bytes 2097152
  115.0 2.3 %copy.33 = f32[2048,128]{1,0:T(8,128)} copy(f32[2048,128]{1,0:T(8,128)} %get-tuple-element.40) | data formatting | bytes 2097152
  117.3 0.0 copy-done.1
  117.3 1.0 copy.34
  118.2 0.0 copy-done
  118.2 2.0 %copy.35 = bf16[2048,1024]{1,0:T(8,128)(2,1)} copy(bf16[2048,1024]{1,0:T(8,128)(2,1)S(1)} %bitcast.15) | data formatting | bytes 8388608
Async XLA Ops:
  4.0 103.6 %copy-start.2 = (f32[16,1024]{1,0:T(8,128)S(1)}, f32[16,1024]{1,0:T(8,128)}, u32[]{:S(2)}) copy-start(f32[16,1024]{1,0:T(8,128)} %master.1) | copy-start | bytes 196612
  4.0 103.6 %copy-start.3 = (f32[16,1024]{1,0:T(8,128)S(1)}, f32[16,1024]{1,0:T(8,128)}, u32[]{:S(2)}) copy-start(f32[16,1024]{1,0:T(8,128)} %m_in.1) | copy-start | bytes 196612
  4.0 103.6 %copy-start.4 = (f32[16,1024]{1,0:T(8,128)S(1)}, f32[16,1024]{1,0:T(8,128)}, u32[]{:S(2)}) copy-start(f32[16,1024]{1,0:T(8,128)} %v_in.1) | copy-start | bytes 196612
  107.6 9.6 %copy-start.1 = (f32[2048,128]{1,0:T(8,128)S(1)}, f32[2048,128]{1,0:T(8,128)}, u32[]{:S(2)}) copy-start(f32[2048,128]{1,0:T(8,128)} %get-tuple-element.41) | copy-start | bytes 3145732
  107.6 10.6 %copy-start = (bf16[4,4,4,2,16,1024]{5,4,3,2,1,0:T(8,128)(2,1)S(1)}, bf16[4,4,4,2,16,1024]{5,4,3,2,1,0:T(8,128)(2,1)}, u32[]{:S(2)}) copy-start(bf16[4,4,4,2,16,1024]{5,4,3,2,1,0:T(8,128)(2,1)} %get-tuple-element.22) | copy-start | bytes 12582916

commit v7 on v6

--- a/solution.py
+++ b/solution.py
@@ -111,7 +111,7 @@
     table, x_all, mix_all, grad, pair, part, bias_part = rest[34:41]
     cold, returned, wide, flat, total, bias_sum, bias_got = rest[41:48]
     mid = rest[58]
-    stage_send, stage_recv, far_sem = rest[59:]
+    stage_send, stage_recv, far_sem, turned_rows = rest[59:]
     send_sem, recv_sem, load_sem = rest[48:51]
     list_send, list_recv, row_send, row_recv, cold_send, cold_recv, own_sem = rest[51:58]
     f32, bf16 = jnp.float32, jnp.bfloat16
@@ -171,9 +171,11 @@
             code = jnp.where(which == 0, f + 1.0, sample).astype(bf16)
             acc = acc + lax.dot_general(code, mask, nt, preferred_element_type=f32)
         found = ((acc[0:1] - 1.0) * samples + acc[1:2]).astype(jnp.int32)
-        inverse_row[:, pl.ds(pl.multiple_of(t * 256, 256), 256)] = jnp.where(
+        found = jnp.where(
             acc[0:1] > 0.5, jnp.clip(found, 0, fields * samples), fields * samples
         )
+        inverse_row[pl.ds(2 * t, 1), :] = found[:, :count]
+        inverse_row[pl.ds(2 * t + 1, 1), :] = found[:, count:]
         return carry
 
     mid[plane] = lists[plane]
@@ -202,7 +204,8 @@
     turned = jnp.clip(turned, 0, cold_table.shape[0] - 1)
     for j in range(cap):
         spread_rows[:, j * count : (j + 1) * count] = turned[j : j + 1, :]
-    read = pltpu.make_async_copy(spread_rows, asked, far_sem)
+    turned_rows[...] = turned[:cap]
+    read = pltpu.make_async_copy(turned_rows, asked, far_sem)
     read.start()
     read.wait()
 
@@ -223,7 +226,7 @@
 
     def pick_row(other, k):
         for j in range(cap):
-            block[k, pl.ds(j, 1), :] = cold_table[pl.ds(asked[0, j * count + other], 1), :]
+            block[k, pl.ds(j, 1), :] = cold_table[pl.ds(asked[j, other], 1), :]
         picked[other] = block[k].astype(bf16)
 
     all_rows = exchange(pick_row, picked, arrived, row_send, row_recv)
@@ -381,9 +384,8 @@
     collect_bias(0)
 
     def pick_grad(other, k):
-        base = other * cap
         for j in range(cap):
-            block[k, pl.ds(j, 1), :] = grad[pl.ds(inverse[0, base + j], 1), :]
+            block[k, pl.ds(j, 1), :] = grad[pl.ds(inverse[j, other], 1), :]
         cold[other] = block[k].astype(bf16)
 
     def hot_tile(t, carry):
@@ -448,29 +450,34 @@
 
         lax.fori_loop(0, cold_table.shape[0] // 256, update_tile, 0)
 
-    for phase in range(4):
-        for k, (low, high) in enumerate(CUTS):
-            order = ORDERS[k]
+    def region_of(k, spread, where):
+        low, high = CUTS[k]
+        at = tuple(slice(None) if a in spread else where[a] for a in range(3))
+        at = at + (core, slice(None))
+        return dense_out.at[at + (slice(low, high),)] if high <= dense else hot_out.at[at]
+
+    for phase in range(3):
+        for k in range(COLORS):
             for copy in waiting[k] if phase else []:
                 copy.wait_recv()
-            spread = order[3 - phase :]
-            at = tuple(slice(None) if a in spread else place[a] for a in range(3))
-            at = at + (core, slice(None))
-            region = dense_out.at[at + (slice(low, high),)] if high <= dense else hot_out.at[at]
-            if phase < 3:
-                axis = order[2 - phase]
-                waiting[k] = [
-                    send(
-                        region, region, k, 4 + phase, s - 1, device_of(moved(place, axis, s), core)
-                    )
-                    for s in (1, 2, 3)
-                ]
-            else:
-                waiting[k] = [send(region, region, k, 7, 0, partner)]
-        if phase == 2:
-            update_cold()
+            region = region_of(k, ORDERS[k][3 - phase :], place)
+            axis = ORDERS[k][2 - phase]
+            waiting[k] = [
+                send(region, region, k, 4 + phase, s - 1, device_of(moved(place, axis, s), core))
+                for s in (1, 2, 3)
+            ]
+            if phase == 2:
+                crossing = [send(region, region, k, 0, 1, partner)]
+                waiting[k] = (waiting[k], crossing)
+    update_cold()
+    for s in (1, 3, 2):
+        for k in range(COLORS):
+            waiting[k][0][s - 1].wait_recv()
+            axis = ORDERS[k][0]
+            region = region_of(k, ORDERS[k][1:], moved(place, axis, 4 - s))
+            waiting[k][1].append(send(region, region, k, 7, s - 1, partner))
     for k in range(COLORS):
-        for copy in waiting[k]:
+        for copy in waiting[k][1]:
             copy.wait_recv()
     for copy in started:
         copy.wait_send()
@@ -513,14 +520,14 @@
             pltpu.VMEM(up.shape, bf16),
             pltpu.VMEM(cold_m.shape, f32),
             pltpu.VMEM(cold_v.shape, f32),
-            pltpu.SMEM((1, count * cap), i32),
-            pltpu.SMEM((1, count * cap), i32),
+            pltpu.SMEM((cap, count), i32),
+            pltpu.SMEM((cap, count), i32),
             pltpu.VMEM((16, 8, 1, emb), i32),
             pltpu.VMEM((count, cap, emb), bf16),
             pltpu.VMEM((count, cap, emb), bf16),
             pltpu.VMEM((8, cap, emb), f32),
             pltpu.VMEM((1, count * cap), i32),
-            pltpu.VMEM((1, count * cap), i32),
+            pltpu.VMEM((cap, count), i32),
             pltpu.VMEM((hot_rows + count * cap, emb), f32),
             pltpu.VMEM((samples, width), bf16),
             pltpu.VMEM((samples, width), bf16),
@@ -541,7 +548,8 @@
         ]
         + [pltpu.SemaphoreType.DMA(())] * 7
         + [pltpu.VMEM((16, 8, 1, emb), i32)]
-        + [pltpu.SemaphoreType.DMA(())] * 3,
+        + [pltpu.SemaphoreType.DMA(())] * 3
+        + [pltpu.VMEM((cap, count), i32)],
         compiler_params=pltpu.CompilerParams(
             collective_id=0, has_side_effects=True, vmem_limit_bytes=60 * 2**20
         ),
@@ -565,6 +573,7 @@
     lookup_slot,
     fetch_rows,
 ):
+    owners, cap = fetch_rows.shape[1:]
     hot_rows = hot_table.shape[0]
     cross_width = cross_down.shape[0]
     is_hot = lookup_slot < 0
@@ -573,7 +582,7 @@
     new_weights, hot_grad, bias_grad, total, cold_new, cold_m_new, cold_v_new = step_all(
         lookup_rows,
         fetch_rows[0],
-        lookup_slot.T,
+        jnp.where(is_hot, -1, lookup_slot % cap * owners + lookup_slot // cap).T,
         hot_only,
         hot_table,
         cold_table,

time: 121 us -> 121 us (level)
  no operation moved by 1% of the time
where the time goes in v7:
time: 121 us; the launch traced here: 120 us
  Pallas kernels  104 us (86%)
  local copies, waits for them, and re-layouts  10.9 us (9%)
  other arithmetic  5.13 us (4%)
    pallas_call x1, Pallas kernels, step_all(): pl.pallas_call(step_kernel, out_shape=(jax.ShapeDtypeStruct((4, 4, 4, 2,...  104 us
    unnamed x17, local copies, waits for them, and re-layouts  10.2 us

profile of v7, /device:TPU:1, one launch (start us, length us, event | category | flops | bytes accessed | tf_op | source)
XLA Modules:
  0.0 120.3 jit_solution(7734141202061104122)
XLA Ops:
  0.6 1.4 %select_bitcast_fusion = (s32[16,256]{1,0:T(8,128)}, s32[2,2,8,128]{3,2,1,0:T(8,128)S(1)}, s32[16,256]{1,0:T(8,128)}) fusion(s32[256,16]{0,1:T(8,128)} %param.25, s32[256,16]{0,1:T(8,128)} %param.26), kind=kLoop, calls=%fused_computation.10 | loop fusion | flops 77824 | bytes 81920 | tf_op jit(solution)/shard_map/transpose | solution.py:581
  2.0 0.6 copy.25
  2.6 0.8 copy.24
  3.4 0.6 pad.4.clone
  4.1 0.0 copy-start.2
  4.1 0.0 copy-start.3
  4.1 0.0 copy-start.4
  4.1 103.6 %step_all.1 = (bf16[4,4,4,2,16,1024]{5,4,3,2,1,0:T(8,128)(2,1)}, bf16[4,4,4,2,16,128]{5,4,3,2,1,0:T(8,128)(2,1)}, f32[1,2048]{1,0:T(1,128)}, f32[16,1024]{1,0:T(...) custom-call(s32[4096]{0:T(1024)} %bitcast.18, s32[16,8,1,128]{3,2,1,0:T(1,128)} %bitcast.17, ...), custom_call_target="tpu_custom_call" | custom-call | tf_op jit(solution)/shard_map/step_all/pallas_call | solution.py:501
  107.7 0.0 copy-start.1
  107.7 0.0 copy-start
  107.7 0.0 copy-done.2
  107.7 0.0 copy-done.3
  107.7 0.0 copy-done.4
  107.8 1.7 %divide_subtract_fusion = (f32[16,1024]{1,0:T(8,128)}, f32[16,1024]{1,0:T(8,128)}, f32[16,1024]{1,0:T(8,128)}) fusion(f32[16,1024]{1,0:T(8,128)S(1)} %copy-done.2, f32[16,1024]{1,0:T(8,128)} %get-tuple-element.21, f32[16,1024]{1,0:T(8,128)S(1)} %copy-done.3, f32[16,1024]{1,0:T(8,128)S(1)} %copy-done.4), kind=kLoop, calls=%fused_computation.1 | loop fusion | flops 212992 | bytes 458752 | tf_op jit(solution)/shard_map/sub | solution.py:21
  109.4 2.1 %bitcast_convert_fusion = f32[2048,128]{1,0:T(8,128)} fusion(bf16[4,4,4,2,16,128]{5,4,3,2,1,0:T(8,128)(2,1)} %get-tuple-element.16), kind=kLoop, calls=%fused_computation | loop fusion | flops 262144 | bytes 1572864 | tf_op jit(solution)/shard_map/convert_element_type | solution.py:600
  111.5 1.3 %copy.31 = f32[2048]{0:T(1024)} copy(f32[2048]{0:T(1024)} %bitcast.20) | data formatting | bytes 16384
  112.8 2.3 %copy.32 = f32[2048,128]{1,0:T(8,128)} copy(f32[2048,128]{1,0:T(8,128)} %get-tuple-element.40) | data formatting | bytes 2097152
  115.1 2.3 %copy.33 = f32[2048,128]{1,0:T(8,128)} copy(f32[2048,128]{1,0:T(8,128)} %get-tuple-element.41) | data formatting | bytes 2097152
  117.3 0.0 copy-done.1
  117.3 1.0 copy.34
  118.3 0.0 copy-done
  118.3 2.0 %copy.35 = bf16[2048,1024]{1,0:T(8,128)(2,1)} copy(bf16[2048,1024]{1,0:T(8,128)(2,1)S(1)} %bitcast.16) | data formatting | bytes 8388608
Async XLA Ops:
  4.1 103.7 %copy-start.2 = (f32[16,1024]{1,0:T(8,128)S(1)}, f32[16,1024]{1,0:T(8,128)}, u32[]{:S(2)}) copy-start(f32[16,1024]{1,0:T(8,128)} %master.1) | copy-start | bytes 196612
  4.1 103.7 %copy-start.3 = (f32[16,1024]{1,0:T(8,128)S(1)}, f32[16,1024]{1,0:T(8,128)}, u32[]{:S(2)}) copy-start(f32[16,1024]{1,0:T(8,128)} %m_in.1) | copy-start | bytes 196612
  4.1 103.7 %copy-start.4 = (f32[16,1024]{1,0:T(8,128)S(1)}, f32[16,1024]{1,0:T(8,128)}, u32[]{:S(2)}) copy-start(f32[16,1024]{1,0:T(8,128)} %v_in.1) | copy-start | bytes 196612
  107.7 9.6 %copy-start.1 = (f32[2048,128]{1,0:T(8,128)S(1)}, f32[2048,128]{1,0:T(8,128)}, u32[]{:S(2)}) copy-start(f32[2048,128]{1,0:T(8,128)} %get-tuple-element.42) | copy-start | bytes 3145732
  107.7 10.6 %copy-start = (bf16[4,4,4,2,16,1024]{5,4,3,2,1,0:T(8,128)(2,1)S(1)}, bf16[4,4,4,2,16,1024]{5,4,3,2,1,0:T(8,128)(2,1)}, u32[]{:S(2)}) copy-start(bf16[4,4,4,2,16,1024]{5,4,3,2,1,0:T(8,128)(2,1)} %get-tuple-element.22) | copy-start | bytes 12582916
